TPU v7x, 32 devices: a whole 2x2x4 slice. The times are simulated.
32 devices in a mesh: ao: 4 (over z), gen: 4 (over y, core), act: 2 (over x).
Axes of the slice: x: 2, y: 2, z: 4, core: 2. Of those that a mesh axis runs over, the one named last changes fastest.
Arguments:
- integrals: bfloat16 [384, 2, 128, 1152], P(('ao', 'gen', 'act')), may hold values from -6 to 6
- bra_rows: bfloat16 [384, 2, 128, 16], P(('ao', 'gen', 'act')), may hold values from -0.02734375 to 0.02734375
- ket_rows: bfloat16 [384, 2, 128, 48], P(('ao', 'gen', 'act')), may hold values from -6 to 6
- block_count: int32 [32], P(('ao', 'gen', 'act')), may hold values from 1 to 12, as said below
- pair_count: int32 [384], P(('ao', 'gen', 'act')), may hold values from 32 to 128
Outputs:
- transformed: float32 [2, 16, 48, 1152], P(None, 'gen', 'act', 'ao')
Inputs may be any that keep to these rules, and one draw needn't show every extreme that they name: `block_count`: one device holds exactly 12 live blocks. Rows from pair_count on are padding.
All inputs are finite; a program needn't handle non-finite values.
Results may differ from a plain program's by a relative error of at most 0.0042.
Values may be sent and summed in bfloat16 or wider, within the bound.
No kernel may reach another device: no remote copies, remote signals or barrier semaphores. Data moves between devices by JAX's collectives and lax.ppermute only.
A program may use at most 128 MiB of HBM per device.

v0:
```python
import jax
import jax.numpy as jnp
from jax import lax
from jax.sharding import PartitionSpec as P


def block_product(ints_block, bra_block, ket_block):
    bra_wide = bra_block.astype(jnp.float32)
    ket_wide = ket_block.astype(jnp.float32)
    real_part = (
        bra_wide[0][:, :, None] * ket_wide[0][:, None, :]
        + bra_wide[1][:, :, None] * ket_wide[1][:, None, :]
    )
    imag_part = (
        bra_wide[0][:, :, None] * ket_wide[1][:, None, :]
        - bra_wide[1][:, :, None] * ket_wide[0][:, None, :]
    )
    rows = bra_block.shape[1]
    real_low = real_part.reshape(rows, -1).T.astype(jnp.bfloat16)
    imag_low = imag_part.reshape(rows, -1).T.astype(jnp.bfloat16)
    upper = jnp.concatenate([real_low, -imag_low], axis=1)
    lower = jnp.concatenate([imag_low, real_low], axis=1)
    weights = jnp.concatenate([upper, lower], axis=0)
    stacked = ints_block.reshape(2 * rows, -1)
    return jnp.dot(weights, stacked, preferred_element_type=jnp.float32)


def local(integrals, bra_rows, ket_rows, block_count, pair_count):
    blocks = integrals.shape[0]
    pair_width = integrals.shape[2]
    columns = integrals.shape[3]
    general = bra_rows.shape[3]
    active = ket_rows.shape[3]
    pair_mask = (jnp.arange(pair_width, dtype=jnp.int32)[None, :] < pair_count[:, None]).astype(
        jnp.bfloat16
    )
    block_live = (jnp.arange(blocks, dtype=jnp.int32) < block_count[0]).astype(jnp.bfloat16)
    masked_ket = ket_rows * pair_mask[:, None, :, None] * block_live[:, None, None, None]
    init = jnp.zeros((2 * general * active, columns), jnp.float32)

    def accumulate(step_number, totals):
        ints_block = lax.dynamic_index_in_dim(integrals, step_number, 0, keepdims=False)
        bra_block = lax.dynamic_index_in_dim(bra_rows, step_number, 0, keepdims=False)
        ket_block = lax.dynamic_index_in_dim(masked_ket, step_number, 0, keepdims=False)
        return totals + block_product(ints_block, bra_block, ket_block)

    totals = lax.fori_loop(0, block_count[0], accumulate, init)
    partial_value = totals.reshape(2, general, active, columns)
    ao_size = lax.axis_size("ao")
    gen_size = lax.axis_size("gen")
    act_size = lax.axis_size("act")
    arranged = partial_value.reshape(
        2, gen_size, general // gen_size, act_size, active // act_size, ao_size, columns // ao_size
    )
    arranged = jnp.transpose(arranged, (5, 1, 3, 0, 2, 4, 6))
    arranged = arranged.reshape(
        ao_size * gen_size * act_size * 2,
        general // gen_size,
        active // act_size,
        columns // ao_size,
    )
    reduced = lax.psum_scatter(arranged, ("ao", "gen", "act"), scatter_dimension=0, tiled=True)
    return reduced


def solution(mesh):
    in_specs = (
        P(("ao", "gen", "act"), None, None, None),
        P(("ao", "gen", "act"), None, None, None),
        P(("ao", "gen", "act"), None, None, None),
        P(("ao", "gen", "act")),
        P(("ao", "gen", "act")),
    )
    out_specs = P(None, "gen", "act", "ao")
    return jax.shard_map(local, mesh=mesh, in_specs=in_specs, out_specs=out_specs, check_vma=False)
```

profile of v0, /device:TPU:0, one launch (start us, length us, event | category | flops | bytes accessed | tf_op | source)
XLA Modules:
  0.0 291.3 jit_solution(10164040220164319253)
XLA Ops:
  6.5 0.0 reduce-scatter.2.cloned.1.call-start
  7.2 0.7 fusion.8
  7.9 1.1 multiply_multiply_fusion
  9.0 3.3 %broadcast_in_dim.2 = f32[1536,1152]{1,0:T(8,128)} broadcast(f32[]{:T(128)} %constant.19.clone.1), dimensions={} | broadcast | bytes 7077892 | tf_op jit(solution)/shard_map/broadcast_in_dim | solution.py:39
  12.3 10.4 %while.10 = (s32[]{:T(128)}, f32[1536,1152]{1,0:T(8,128)}, s32[]{:T(128)}, bf16[12,2,128,16]{2,3,1,0:T(8,128)(2,1)}, bf16[12,2,128,48]{2,3,1,0:T(8,128)(2,1)S(1)...) while((s32[]{:T(128)}, f32[1536,1152]{1,0:T(8,128)}, s32[]{:T(128)}, ...), condition=%wide.region_1.2_spmd, body=%wide.region_0.1_spmd.sunk | while | flops 911785984 | bytes 17596564 | solution.py:47
  13.0 0.7 dynamic-slice_convert_fusion.5
  13.7 0.1 subtract_convert_fusion.2
  13.9 1.1 constant_dynamic-slice_fusion.2
  15.0 7.0 %convolution_add_fusion.2 = f32[1536,1152]{1,0:T(8,128)} fusion(f32[1536,1152]{1,0:T(8,128)} %get-tuple-element.117, bf16[256,1152]{1,0:T(8,128)(2,1)S(1)} %bitcast.36, bf16[768,128]{1,0:T(8,128)(2,1)S(1)} %bitcast.39, bf16[768,128]{1,0:T(8,128)(2,1)S(1)} %bitcast.37, bf16[768,128]{1,0:T(8,128)(2,1)S(1)} %bitcast_negate_fusion.2), kind=kOutput, calls=%fused_computation.clone.1 | convolution fusion | flops 910884864 | bytes 15335424 | tf_op jit(solution)/shard_map/while/body/dot_general | solution.py:25
  22.7 11.1 %reshape_reshape.3 = f32[2,4,4,2,24,4,288]{6,5,4,3,2,1,0:T(4,128)} reshape(f32[1536,1152]{1,0:T(8,128)} %get-tuple-element.38) | data formatting | bytes 14155776 | tf_op jit(solution)/shard_map/reshape;reshape | solution.py:52
  33.7 8.6 %copy.10 = f32[2,4,4,2,24,4,288]{6,4,2,0,3,1,5:T(8,128)} copy(f32[2,4,4,2,24,4,288]{6,5,4,3,2,1,0:T(4,128)} %reshape_reshape.3) | data formatting | bytes 14155776 | tf_op jit(solution)/shard_map/reshape;reshape | solution.py:52
  42.4 0.0 reduce-scatter.2.cloned.1.call-update
  42.4 242.1 %reduce-scatter.2.cloned.1.call-done = f32[2,4,24,288]{3,2,1,0:T(8,128)} async-done(((f32[64,4,24,288]{3,2,1,0:T(8,128)}), f32[2,4,24,288]{3,2,1,0:T(8,128)}) %reduce-scatter.2.cloned.1.call-update) | async-done | bytes 221200 | tf_op jit(solution)/shard_map/reduce_scatter | solution.py:62
  (5 shorter events, 0.1 us)
Async XLA Ops:
  6.5 277.9 %reduce-scatter.2.cloned.1.call-start = ((), (), s32[]{:S(2)}) async-start(), calls=%async_computation.1 | async-start | bytes 9732096 | tf_op jit(solution)/shard_map/reduce_scatter | solution.py:62
Sparse Core Ops, SparseCore 0:
  42.5 241.9 reduce-scatter.1
where the time goes:
time: 294 us; the launch traced here: 291 us
  waiting for transfers between devices  242 us (82%)
  local copies, waits for them, and re-layouts  24.1 us (8%)
  between operations  14.1 us (5%)
  matrix products  7.05 us (2%)
    reduce_scatter x1, waiting for transfers between devices, local(): lax.psum_scatter(arranged, ('ao', 'gen', 'act'), scatter_dimension=0, til...  242 us
    another operation x2, local copies, waits for them, and re-layouts, local(): partial_value.reshape(2, gen_size, general // gen_size, act_size, active...  19.7 us
    dot_general x1, matrix products, block_product(): return jnp.dot(weights, stacked, preferred_element_type=jnp.float32)  7.05 us
  transfers between devices with their start and end apart: 1, of which 1 were waited for; matrix products, arithmetic and copies ran while one was open for 0% of the time, Pallas kernels for 0%

commit v1 on v0

v1 whole, which is shorter than its diff:
```python
import functools

import jax
import jax.numpy as jnp
from jax import lax
from jax.experimental import pallas as pl
from jax.experimental.pallas import tpu as pltpu
from jax.sharding import PartitionSpec as P


LANES = 128
GRAIN = 16
STEP = 2
GRANT = 48 * 2**20
PARTS = (1, 1)


def parts_of(p_own):
    if p_own % sum(PARTS):
        return (p_own,)
    return tuple(p_own // sum(PARTS) * part for part in PARTS)


def blocks_of(dims, chunk):
    general, _, gen_size, act_size = dims
    parts = parts_of(general // gen_size)
    p_from = sum(parts[:chunk])
    return [
        (g, a, p_from, p_from + parts[chunk])
        for parity in (1, 0)
        for g in range(parity, gen_size, 2)
        for a in range(act_size)
    ]


def make_weights(dims, chunk, t, column, bra_pack, ket_pack, weights):
    general, active, gen_size, act_size = dims
    p_own, u_own = general // gen_size, active // act_size
    me_gen, me_act = lax.axis_index("gen"), lax.axis_index("act")
    left, right = slice(column, column + LANES), slice(column + LANES, column + 2 * LANES)
    row = 0
    for g, a, p_from, p_to in blocks_of(dims, chunk):
        p_first = (me_gen ^ g) * p_own
        u_first = pl.multiple_of((me_act ^ a) * u_own, 8)
        ket_re = ket_pack[t, pl.ds(u_first, u_own), :]
        ket_im = ket_pack[t, pl.ds(active + u_first, u_own), :]
        real, imag = [], []
        for p in range(p_from, p_to):
            bra_re = bra_pack[t, pl.ds(p_first + p, 1), :]
            bra_im = bra_pack[t, pl.ds(general + p_first + p, 1), :]
            real.append(bra_re * ket_re + bra_im * ket_im)
            imag.append(bra_re * ket_im - bra_im * ket_re)
        rows = 2 * (p_to - p_from) * u_own
        first = jnp.concatenate(real + imag, axis=0).astype(jnp.bfloat16)
        second = jnp.concatenate([-x for x in imag] + real, axis=0).astype(jnp.bfloat16)
        weights[row : row + rows, left] = first
        weights[row : row + rows, right] = second
        row += rows


def product_kernel(dims, chunk, blocks, width, counts_ref, *refs):
    outs = 1 + len(blocks_of(dims, chunk)) // 2
    if chunk == 0:
        rows_ref, ints_ref = refs[:2]
        results = refs[2 : 2 + outs]
        bra_pack, ket_pack = refs[2 + outs : 4 + outs]
    else:
        bra_pack, ket_pack, ints_ref = refs[:3]
        results = refs[3 : 3 + outs]
    packed, weights, acc, offsets, sems = refs[-5:]
    general = dims[0]
    live = counts_ref[blocks]

    def rows_of(b):
        return (counts_ref[b] + GRAIN - 1) // GRAIN * GRAIN

    pieces = []
    size = width
    while size >= GRAIN:
        pieces.append(size)
        size //= 2

    def copies(b, act):
        rows = rows_of(b)
        start = pl.multiple_of(offsets[b], GRAIN)
        for piece in pieces:
            @pl.when((rows & piece) != 0)
            def _():
                first = pl.multiple_of(rows & ~(2 * piece - 1), GRAIN)
                copy = pltpu.make_async_copy(
                    ints_ref.at[b, :, pl.ds(first, piece), :],
                    packed.at[:, pl.ds(start + first, piece), :],
                    sems.at[b],
                )
                act(copy)

    def place(b, total):
        offsets[b] = total
        copies(b, lambda c: c.start())
        return total + rows_of(b)

    total = lax.fori_loop(0, live, place, 0)
    steps = (total + STEP * LANES - 1) // (STEP * LANES)

    def clear(i, _):
        row = pl.multiple_of(total + i * GRAIN, GRAIN)
        packed[:, pl.ds(row, GRAIN), :] = jnp.zeros((2, GRAIN, packed.shape[2]), packed.dtype)
        return 0

    lax.fori_loop(0, (steps * STEP * LANES - total) // GRAIN, clear, 0)

    if chunk == 0:
        @pl.loop(0, steps * STEP + 1)
        def _(t):
            bra_pack[t] = jnp.zeros(bra_pack.shape[1:], jnp.float32)
            ket_pack[t] = jnp.zeros(ket_pack.shape[1:], jnp.float32)

        lane = lax.broadcasted_iota(jnp.int32, (1, LANES), 1)
        for b in range(blocks):
            start = jnp.where(b < live, offsets[b], 0)
            rows = jnp.where(b < live, counts_ref[b], 0)
            tile = start // LANES
            turn = start % LANES
            both = rows_ref[b].astype(jnp.float32)
            for first, last, target in ((0, general, bra_pack), (general, both.shape[1], ket_pack)):
                value = both[:, first:last].reshape(target.shape[1:])
                value = pltpu.roll(jnp.where(lane < rows, value, 0.0), turn, 1)
                target[tile] += jnp.where(lane >= turn, value, 0.0)
                target[tile + 1] += jnp.where(lane < turn, value, 0.0)

    acc[...] = jnp.zeros_like(acc)

    def product(i, ready):
        for k in range(STEP):
            make_weights(
                dims, chunk, i * STEP + k, 2 * LANES * k, bra_pack, ket_pack, weights
            )

        def pending(b):
            start = offsets[jnp.minimum(b, blocks - 1)]
            return jnp.logical_and(b < live, start < (i + 1) * STEP * LANES)

        def arrive(b):
            copies(b, lambda c: c.wait())
            return b + 1

        ready = lax.while_loop(pending, arrive, ready)
        values = []
        for k in range(STEP):
            first = pl.multiple_of((i * STEP + k) * LANES, LANES)
            values.append(packed[0, pl.ds(first, LANES), :])
            values.append(packed[1, pl.ds(first, LANES), :])
        values = jnp.concatenate(values, axis=0)
        return jnp.dot(weights[...], values, preferred_element_type=jnp.float32), ready

    def step(i, ready):
        value, ready = product(i, ready)
        acc[...] += value
        return ready

    ready = lax.fori_loop(0, steps - 1, step, 0)
    value, _ = product(steps - 1, ready)
    value = acc[...] + value
    row = 0
    for result in results:
        result[...] = value[row : row + result.shape[0]].astype(result.dtype)
        row += result.shape[0]


SMEM = pl.BlockSpec(memory_space=pltpu.SMEM)
VMEM = pl.BlockSpec(memory_space=pltpu.VMEM)
HBM = pl.BlockSpec(memory_space=pltpu.HBM)


def products(dims, chunk, counts, operands, integrals):
    general, active, _, act_size = dims
    blocks, _, width, columns = integrals.shape
    u_own = active // act_size
    tiles = -(-blocks * width // (STEP * LANES)) * STEP
    sizes = [2 * (p_to - p_from) * u_own for _, _, p_from, p_to in blocks_of(dims, chunk)]
    rows = sum(sizes)
    outs = [jax.ShapeDtypeStruct((rows // 2, columns), jnp.bfloat16)]
    outs += [
        jax.ShapeDtypeStruct((size, columns), jnp.float32) for size in sizes[len(sizes) // 2 :]
    ]
    if chunk == 0:
        outs += [
            jax.ShapeDtypeStruct((tiles + 1, 2 * general, LANES), jnp.float32),
            jax.ShapeDtypeStruct((tiles + 1, 2 * active, LANES), jnp.float32),
        ]
    return pl.pallas_call(
        functools.partial(product_kernel, dims, chunk, blocks, width),
        out_shape=outs,
        in_specs=[SMEM] + [VMEM] * len(operands) + [HBM],
        out_specs=[VMEM] * len(outs),
        scratch_shapes=[
            pltpu.VMEM((2, tiles * LANES, columns), jnp.bfloat16),
            pltpu.VMEM((rows, 2 * STEP * LANES), jnp.bfloat16),
            pltpu.VMEM((rows, columns), jnp.float32),
            pltpu.SMEM((blocks,), jnp.int32),
            pltpu.SemaphoreType.DMA((blocks,)),
        ],
        compiler_params=pltpu.CompilerParams(vmem_limit_bytes=GRANT),
        cost_estimate=pl.CostEstimate(
            flops=rows * columns * 2 * blocks * LANES,
            bytes_accessed=rows * columns * 3,
            transcendentals=0,
        ),
    )(counts, *operands, integrals)


def window_of(columns, parts):
    own = columns // parts
    starts = [own * a // LANES * LANES for a in range(parts)]
    ends = [-(-own * (a + 1) // LANES) * LANES for a in range(parts)]
    width = max(e - s for s, e in zip(starts, ends))
    return own, width, [min(s, columns - width) for s in starts]


def choose(index, values):
    result = values[0]
    for i in range(1, len(values)):
        result = jnp.where(index == i, values[i], result)
    return result


def swap(size, bit):
    return [(i, i ^ bit) for i in range(size)]


def local(integrals, bra_rows, ket_rows, block_count, pair_count):
    columns = integrals.shape[3]
    general, active = bra_rows.shape[3], ket_rows.shape[3]
    ao_size = lax.axis_size("ao")
    gen_size = lax.axis_size("gen")
    act_size = lax.axis_size("act")
    me_ao = lax.axis_index("ao")
    bra = jnp.swapaxes(bra_rows, 2, 3)
    ket = jnp.swapaxes(ket_rows, 2, 3)
    p_own, u_own = general // gen_size, active // act_size
    dims = (general, active, gen_size, act_size)
    counts = jnp.concatenate([pair_count, block_count])
    operands = (jnp.concatenate([bra, ket], axis=2),)
    own, width, starts = window_of(columns, ao_size)
    outs = []
    kept = gen_size // 2 * act_size
    for chunk, part in enumerate(parts_of(p_own)):
        block = 2 * part * u_own
        send, *keep = products(dims, chunk, counts, operands, integrals)
        if chunk == 0:
            operands = tuple(keep[kept:])
        got = lax.ppermute(send, "gen", swap(gen_size, 1))
        index = 0
        for g in range(0, gen_size, 2):
            for a in range(act_size):
                piece = keep[index] + got[index * block : (index + 1) * block].astype(jnp.float32)
                index += 1
                if g == 0 and a == 0:
                    total = piece
                    continue
                pairs = [
                    (i * act_size + k, (i ^ g) * act_size + (k ^ a))
                    for i in range(gen_size)
                    for k in range(act_size)
                ]
                low = piece.astype(jnp.bfloat16)
                arrived = lax.ppermute(low, ("gen", "act"), pairs)
                total = total + arrived.astype(jnp.float32)
        if ao_size <= 4:
            windows = [total[:, s : s + width] for s in starts]
            value = choose(me_ao, windows)
            for k in range(1, ao_size):
                cut = choose(me_ao ^ k, windows).astype(jnp.bfloat16)
                arrived = lax.ppermute(cut, "ao", swap(ao_size, k))
                value = value + arrived.astype(jnp.float32)
            shifts = [own * a - starts[a] for a in range(ao_size)]
            value = choose(me_ao, [value[:, s : s + own] for s in shifts])
        else:
            total = total.reshape(block, ao_size, own)
            total = jnp.swapaxes(total, 0, 1).reshape(ao_size * block, own)
            value = lax.psum_scatter(total, "ao", scatter_dimension=0, tiled=True)
        outs.append(value.reshape(2, part, u_own, own))
    return jnp.concatenate(outs, axis=1)


def swap(size, bit):
    return [(i, i ^ bit) for i in range(size)]


def solution(mesh):
    spec = P(("ao", "gen", "act"), None, None, None)
    count = P(("ao", "gen", "act"))

    def program(integrals, bra_rows, ket_rows, block_count, pair_count):
        mapped = jax.shard_map(
            local,
            mesh=mesh,
            in_specs=(spec, spec, spec, count, count),
            out_specs=P(None, "gen", "act", "ao"),
            check_vma=False,
        )
        return mapped(integrals, bra_rows, ket_rows, block_count, pair_count)

    return program
```

time: 294 us -> 60.5 us (0.21)
  waiting for transfers between devices: 242 us -> 16.4 us
  starting transfers between devices: 0.01 us -> 24.5 us
  local copies, waits for them, and re-layouts: 24.1 us -> 0 us
  between operations: 14.1 us -> 0.78 us
  Pallas kernels: 0 us -> 10.7 us
  matrix products: 7.05 us -> 0 us
  other arithmetic: 2.65 us -> 7.75 us
    reduce_scatter x1 -> x0, waiting for transfers between devices: 242 us -> none  [local(): lax.psum_scatter(arranged, ('ao', 'gen', 'act'), scatter_dimension=0, til...]
    ppermute x0 -> x14, starting transfers between devices: none -> 24.5 us  [the longest x6 11.9 us: local(): arrived = lax.ppermute(low, ('gen', 'act'), pairs)]
    another operation x2 -> x0, local copies, waits for them, and re-layouts: 19.7 us -> none  [local(): partial_value.reshape(2, gen_size, general // gen_size, act_size, active...]
    ppermute x0 -> x14, waiting for transfers between devices: none -> 16.4 us  [the longest x6 12.8 us: local(): arrived = lax.ppermute(low, ('gen', 'act'), pairs)]
    pallas_call x0 -> x2, Pallas kernels: none -> 10.7 us  [products(): pl.pallas_call(functools.partial(product_kernel, dims, chunk, blocks, wid...]
    dot_general x1 -> x0, matrix products: 7.05 us -> none  [block_product(): return jnp.dot(weights, stacked, preferred_element_type=jnp.float32)]
    broadcast_in_dim x1 -> x0, local copies, waits for them, and re-layouts: 3.31 us -> none  [local(): init = jnp.zeros((2 * general * active, columns), jnp.float32)]
  transfers between devices with their start and end apart: 1 -> 14, of which waited for: 1 -> 4; matrix products, arithmetic and copies ran while one was open for 0% -> 8% of each run, Pallas kernels for 0% -> 9%
where the time goes in v1:
time: 60.5 us; the launch traced here: 60.2 us
  starting transfers between devices  24.5 us (40%)
  waiting for transfers between devices  16.4 us (27%)
  Pallas kernels  10.7 us (18%)
  other arithmetic  7.75 us (13%)
  between operations  0.78 us (1%)
    ppermute x6, waiting for transfers between devices, local(): arrived = lax.ppermute(low, ('gen', 'act'), pairs)  12.8 us
    ppermute x6, starting transfers between devices, local(): arrived = lax.ppermute(low, ('gen', 'act'), pairs)  11.9 us
    pallas_call x2, Pallas kernels, products(): pl.pallas_call(functools.partial(product_kernel, dims, chunk, blocks, wid...  10.7 us
    ppermute x6, starting transfers between devices, local(): arrived = lax.ppermute(cut, 'ao', swap(ao_size, k))  8.94 us
    ppermute x2, starting transfers between devices, local(): got = lax.ppermute(send, 'gen', swap(gen_size, 1))  3.68 us
    ppermute x6, waiting for transfers between devices, local(): arrived = lax.ppermute(cut, 'ao', swap(ao_size, k))  3.59 us
    convert_element_type x2, other arithmetic, local(): low = piece.astype(jnp.bfloat16)  2.53 us
    add x2, other arithmetic, local(): total = total + arrived.astype(jnp.float32)  2.12 us
  transfers between devices with their start and end apart: 14, of which 4 were waited for; matrix products, arithmetic and copies ran while one was open for 8% of the time, Pallas kernels for 9%

profile of v1, /device:TPU:0, one launch (start us, length us, event | category | flops | bytes accessed | tf_op | source)
XLA Modules:
  0.0 60.2 jit_solution(9923542580031859523)
XLA Ops:
  0.7 0.7 %pad_add_fusion.counts_ref = s32[13]{0:T(128)S(1)} fusion(s32[1]{0:T(128)S(6)} %copy.6, s32[12]{0:T(128)} %param.9), kind=kLoop, calls=%fused_computation.24 | loop fusion | flops 13 | bytes 104 | tf_op jit(solution)/shard_map/concatenate | solution.py:242
  1.4 1.0 %pad_maximum_fusion.refs_0_ = bf16[12,2,64,128]{3,2,1,0:T(8,128)(2,1)S(1)} fusion(bf16[12,2,48,128]{3,2,1,0:T(8,128)(2,1)} %bitcast.6, bf16[12,2,16,128]{3,2,1,0:T(8,128)(2,1)} %bitcast.7), kind=kLoop, calls=%fused_computation.8 | loop fusion | flops 786432 | bytes 786432 | tf_op jit(solution)/shard_map/concatenate | solution.py:243
  2.4 5.4 %shard_map.55 = (bf16[384,1152]{1,0:T(8,128)(2,1)}, f32[96,1152]{1,0:T(8,128)S(1)}, f32[96,1152]{1,0:T(8,128)S(1)}, f32[96,1152]{1,0:T(8,128)S(1)}, f32[96,1152]...) custom-call(s32[13]{0:T(128)S(1)} %pad_add_fusion.counts_ref, ...), custom_call_target="tpu_custom_call" | custom-call | flops 2717908992 | bytes 2654208 | tf_op jit(solution)/shard_map/pallas_call | solution.py:191
  7.8 2.1 %collective-permute-start = (bf16[384,1152]{1,0:T(8,128)(2,1)}, bf16[384,1152]{1,0:T(8,128)(2,1)}, u32[]{:S(2)}, u32[]{:S(2)}) collective-permute-start(bf16[384,1152]{1,0:T(8,128)(2,1)} %get-tuple-element.18), channel_id=1, source_target_pairs={{0,2},{2,0},{4,6},{6,4},{1,3},{3,1},{5,7},{7,5},{8,10},{10,8},{12,... | collective-permute-start | bytes 2654216 | tf_op jit(solution)/shard_map/ppermute | solution.py:252
  9.9 5.3 %shard_map.56 = (bf16[384,1152]{1,0:T(8,128)(2,1)}, f32[96,1152]{1,0:T(8,128)S(1)}, f32[96,1152]{1,0:T(8,128)S(1)}, f32[96,1152]{1,0:T(8,128)S(1)}, f32[96,1152]{1,0:T(8,128)S(1)}) custom-call(s32[13]{0:T(128)S(1)} %pad_add_fusion.counts_ref, f32[13,32,128]{2,1,0:T(8,128)S(1)} %get-tuple-element.22.refs_0_, f32[13,96,128]{2,1,0:T(8,128)S(1)} %get-tuple-element.23.refs_1_, ...), custom_call_target="tpu_custom_call" | custom-call | flops 2717908992 | bytes 2654208 | tf_op jit(solution)/shard_map/pallas_call | solution.py:191
  15.2 1.6 %collective-permute-start.7 = (bf16[384,1152]{1,0:T(8,128)(2,1)}, bf16[384,1152]{1,0:T(8,128)(2,1)}, u32[]{:S(2)}, u32[]{:S(2)}) collective-permute-start(bf16[384,1152]{1,0:T(8,128)(2,1)} %get-tuple-element.25), channel_id=1, source_target_pairs={{0,2},{2,0},{4,6},{6,4},{1,3},{3,1},{5,7},{7,5},{8,10},{10,8},{12,... | collective-permute-start | bytes 2654216 | tf_op jit(solution)/shard_map/ppermute | solution.py:252
  16.8 1.3 %add_convert_fusion.5 = (bf16[96,1152]{1,0:T(8,128)(2,1)S(1)}, bf16[96,1152]{1,0:T(8,128)(2,1)S(1)}, bf16[96,1152]{1,0:T(8,128)(2,1)S(1)}) fusion(f32[96,1152]{1,0:T(8,128)S(1)} %get-tuple-element.19, bf16[384,1152]{1,0:T(8,128)(2,1)} %collective-permute-done, f32[96,1152]{1,0:T(8,128)S(1)} %get-tuple-element.21, f32[96,1152]{1,0:T(8,128)S(1)} %get-tuple-element.20), kind=kLoop, calls=%fused_computation.7 | loop fusion | flops 995328 | bytes 2654208 | tf_op jit(solution)/shard_map/convert_element_type | solution.py:266
  18.1 8.2 %collective-permute-start.1 = (bf16[96,1152]{1,0:T(8,128)(2,1)S(1)}, bf16[96,1152]{1,0:T(8,128)(2,1)S(1)}, u32[]{:S(2)}, u32[]{:S(2)}) collective-permute-start(bf16[96,1152]{1,0:T(8,128)(2,1)S(1)} %get-tuple-element.29), channel_id=1, source_target_pairs={{0,1},{1,0},{2,3},{3,2},{4,5},{5,4},{6,7},{7,6},{8,9},{9,8},{10,11... | collective-permute-start | bytes 663560 | tf_op jit(solution)/shard_map/ppermute | solution.py:267
  26.3 1.5 %collective-permute-start.3 = (bf16[96,1152]{1,0:T(8,128)(2,1)S(1)}, bf16[96,1152]{1,0:T(8,128)(2,1)S(1)}, u32[]{:S(2)}, u32[]{:S(2)}) collective-permute-start(bf16[96,1152]{1,0:T(8,128)(2,1)S(1)} %get-tuple-element.30), channel_id=1, source_target_pairs={{0,5},{1,4},{2,7},{3,6},{4,1},{5,0},{6,3},{7,2},{8,13},{9,12},{10,... | collective-permute-start | bytes 663560 | tf_op jit(solution)/shard_map/ppermute | solution.py:267
  27.8 1.3 %add_convert_fusion.2 = (bf16[96,1152]{1,0:T(8,128)(2,1)S(1)}, bf16[96,1152]{1,0:T(8,128)(2,1)S(1)}, bf16[96,1152]{1,0:T(8,128)(2,1)S(1)}) fusion(f32[96,1152]{1,0:T(8,128)S(1)} %get-tuple-element.26, bf16[384,1152]{1,0:T(8,128)(2,1)} %collective-permute-done.7, f32[96,1152]{1,0:T(8,128)S(1)} %get-tuple-element.28, f32[96,1152]{1,0:T(8,128)S(1)} %get-tuple-element.27), kind=kLoop, calls=%fused_computation.3 | loop fusion | flops 995328 | bytes 2654208 | tf_op jit(solution)/shard_map/convert_element_type | solution.py:266
  29.1 1.5 %collective-permute-start.10 = (bf16[96,1152]{1,0:T(8,128)(2,1)S(1)}, bf16[96,1152]{1,0:T(8,128)(2,1)S(1)}, u32[]{:S(2)}, u32[]{:S(2)}) collective-permute-start(bf16[96,1152]{1,0:T(8,128)(2,1)S(1)} %get-tuple-element.33), channel_id=1, source_target_pairs={{0,5},{1,4},{2,7},{3,6},{4,1},{5,0},{6,3},{7,2},{8,13},{9,12},{10,... | collective-permute-start | bytes 663560 | tf_op jit(solution)/shard_map/ppermute | solution.py:267
  30.5 0.6 %collective-permute-start.8 = (bf16[96,1152]{1,0:T(8,128)(2,1)S(1)}, bf16[96,1152]{1,0:T(8,128)(2,1)S(1)}, u32[]{:S(2)}, u32[]{:S(2)}) collective-permute-start(bf16[96,1152]{1,0:T(8,128)(2,1)S(1)} %get-tuple-element.32), channel_id=1, source_target_pairs={{0,1},{1,0},{2,3},{3,2},{4,5},{5,4},{6,7},{7,6},{8,9},{9,8},{10,11... | collective-permute-start | bytes 663560 | tf_op jit(solution)/shard_map/ppermute | solution.py:267
  31.2 1.4 %collective-permute-done.1 = bf16[96,1152]{1,0:T(8,128)(2,1)S(1)} collective-permute-done((bf16[96,1152]{1,0:T(8,128)(2,1)S(1)}, bf16[96,1152]{1,0:T(8,128)(2,1)S(1)}, u32[]{:S(2)}, u32[]{:S(2)}) %collective-permute-start.1) | collective-permute-done | bytes 221216 | tf_op jit(solution)/shard_map/ppermute | solution.py:267
  32.6 0.1 collective-permute-start.9
  32.7 11.4 %collective-permute-done.2 = bf16[96,1152]{1,0:T(8,128)(2,1)S(1)} collective-permute-done((bf16[96,1152]{1,0:T(8,128)(2,1)S(1)}, bf16[96,1152]{1,0:T(8,128)(2,1)S(1)}, u32[]{:S(2)}, u32[]{:S(2)}) %collective-permute-start.2) | collective-permute-done | bytes 221216 | tf_op jit(solution)/shard_map/ppermute | solution.py:267
  44.1 1.1 %convert_add_fusion.1 = f32[96,1152]{1,0:T(8,128)S(1)} fusion(bf16[96,1152]{1,0:T(8,128)(2,1)S(1)} %collective-permute-done.3, bf16[96,1152]{1,0:T(8,128)(2,1)S(1)} %collective-permute-done.2, bf16[96,1152]{1,0:T(8,128)(2,1)S(1)} %collective-permute-done.1, f32[96,1152]{1,0:T(8,128)S(1)} %get-tuple-element.17, bf16[384,1152]{1,0:T(8,128)(2,1)} %collective-permute-done), kind=kLoop, calls=%fused_computation.4 | loop fusion | flops 884736 | bytes 1769472 | tf_op jit(solution)/shard_map/add | solution.py:268
  45.2 0.1 collective-permute-start.4
  45.3 0.1 collective-permute-start.5
  45.4 0.0 collective-permute-done.10
  45.4 4.4 %collective-permute-start.6 = (bf16[96,384]{1,0:T(8,128)(2,1)S(1)}, bf16[96,384]{1,0:T(8,128)(2,1)S(1)}, u32[]{:S(2)}, u32[]{:S(2)}) collective-permute-start(bf16[96,384]{1,0:T(8,128)(2,1)S(1)} %select_convert_fusion.3), channel_id=1, source_target_pairs={{0,24},{8,16},{16,8},{24,0},{1,25},{9,17},{17,9},{25,1},{2,26},{10... | collective-permute-start | bytes 221192 | tf_op jit(solution)/shard_map/ppermute | solution.py:274
  49.7 1.1 %convert_add_fusion = f32[96,1152]{1,0:T(8,128)S(1)} fusion(bf16[96,1152]{1,0:T(8,128)(2,1)S(1)} %collective-permute-done.10, bf16[96,1152]{1,0:T(8,128)(2,1)S(1)} %collective-permute-done.9, bf16[96,1152]{1,0:T(8,128)(2,1)S(1)} %collective-permute-done.8, f32[96,1152]{1,0:T(8,128)S(1)} %get-tuple-element.24, bf16[384,1152]{1,0:T(8,128)(2,1)} %collective-permute-done.7), kind=kLoop, calls=%fused_computation | loop fusion | flops 884736 | bytes 1769472 | tf_op jit(solution)/shard_map/add | solution.py:268
  50.9 0.1 collective-permute-start.11
  51.0 0.6 collective-permute-start.12
  51.6 3.8 %collective-permute-start.13 = (bf16[96,384]{1,0:T(8,128)(2,1)S(1)}, bf16[96,384]{1,0:T(8,128)(2,1)S(1)}, u32[]{:S(2)}, u32[]{:S(2)}) collective-permute-start(bf16[96,384]{1,0:T(8,128)(2,1)S(1)} %select_convert_fusion), channel_id=1, source_target_pairs={{0,24},{8,16},{16,8},{24,0},{1,25},{9,17},{17,9},{25,1},{2,26},{10... | collective-permute-start | bytes 221192 | tf_op jit(solution)/shard_map/ppermute | solution.py:274
  55.4 0.0 collective-permute-done.5
  55.4 0.1 convert_add_fusion.3
  55.4 0.2 fusion.3
  55.6 1.0 %collective-permute-done.11 = bf16[96,384]{1,0:T(8,128)(2,1)S(1)} collective-permute-done((bf16[96,384]{1,0:T(8,128)(2,1)S(1)}, bf16[96,384]{1,0:T(8,128)(2,1)S(1)}, u32[]{:S(2)}, u32[]{:S(2)}) %collective-permute-start.11) | collective-permute-done | bytes 73760 | tf_op jit(solution)/shard_map/ppermute | solution.py:274
  56.6 2.5 %collective-permute-done.12 = bf16[96,384]{1,0:T(8,128)(2,1)S(1)} collective-permute-done((bf16[96,384]{1,0:T(8,128)(2,1)S(1)}, bf16[96,384]{1,0:T(8,128)(2,1)S(1)}, u32[]{:S(2)}, u32[]{:S(2)}) %collective-permute-start.12) | collective-permute-done | bytes 73760 | tf_op jit(solution)/shard_map/ppermute | solution.py:274
  59.2 0.1 convert_add_fusion.2
  59.2 0.2 fusion.1
  59.4 0.7 %pad_maximum_fusion.1 = f32[2,4,24,288]{3,2,1,0:T(8,128)} fusion(f32[2,2,24,288]{3,2,1,0:T(8,128)S(1)} %bitcast.5, f32[2,2,24,288]{3,2,1,0:T(8,128)S(1)} %bitcast.4), kind=kLoop, calls=%fused_computation.9 | loop fusion | flops 55296 | bytes 442368 | tf_op jit(solution)/shard_map/concatenate | solution.py:283
  (13 shorter events, 0.2 us)
Async XLA Ops:
  7.8 9.0 %collective-permute-start = (bf16[384,1152]{1,0:T(8,128)(2,1)}, bf16[384,1152]{1,0:T(8,128)(2,1)}, u32[]{:S(2)}, u32[]{:S(2)}) collective-permute-start(bf16[384,1152]{1,0:T(8,128)(2,1)} %get-tuple-element.18), channel_id=1, source_target_pairs={{0,2},{2,0},{4,6},{6,4},{1,3},{3,1},{5,7},{7,5},{8,10},{10,8},{12,... | collective-permute-start | bytes 2654216 | tf_op jit(solution)/shard_map/ppermute | solution.py:252
  15.2 12.6 %collective-permute-start.7 = (bf16[384,1152]{1,0:T(8,128)(2,1)}, bf16[384,1152]{1,0:T(8,128)(2,1)}, u32[]{:S(2)}, u32[]{:S(2)}) collective-permute-start(bf16[384,1152]{1,0:T(8,128)(2,1)} %get-tuple-element.25), channel_id=1, source_target_pairs={{0,2},{2,0},{4,6},{6,4},{1,3},{3,1},{5,7},{7,5},{8,10},{10,8},{12,... | collective-permute-start | bytes 2654216 | tf_op jit(solution)/shard_map/ppermute | solution.py:252
  18.1 14.5 %collective-permute-start.1 = (bf16[96,1152]{1,0:T(8,128)(2,1)S(1)}, bf16[96,1152]{1,0:T(8,128)(2,1)S(1)}, u32[]{:S(2)}, u32[]{:S(2)}) collective-permute-start(bf16[96,1152]{1,0:T(8,128)(2,1)S(1)} %get-tuple-element.29), channel_id=1, source_target_pairs={{0,1},{1,0},{2,3},{3,2},{4,5},{5,4},{6,7},{7,6},{8,9},{9,8},{10,11... | collective-permute-start | bytes 663560 | tf_op jit(solution)/shard_map/ppermute | solution.py:267
  26.3 17.8 %collective-permute-start.2 = (bf16[96,1152]{1,0:T(8,128)(2,1)S(1)}, bf16[96,1152]{1,0:T(8,128)(2,1)S(1)}, u32[]{:S(2)}, u32[]{:S(2)}) collective-permute-start(bf16[96,1152]{1,0:T(8,128)(2,1)S(1)} %get-tuple-element.31), channel_id=1, source_target_pairs={{0,4},{1,5},{2,6},{3,7},{4,0},{5,1},{6,2},{7,3},{8,12},{9,13},{10,... | collective-permute-start | bytes 663560 | tf_op jit(solution)/shard_map/ppermute | solution.py:267
  26.3 17.8 %collective-permute-start.3 = (bf16[96,1152]{1,0:T(8,128)(2,1)S(1)}, bf16[96,1152]{1,0:T(8,128)(2,1)S(1)}, u32[]{:S(2)}, u32[]{:S(2)}) collective-permute-start(bf16[96,1152]{1,0:T(8,128)(2,1)S(1)} %get-tuple-element.30), channel_id=1, source_target_pairs={{0,5},{1,4},{2,7},{3,6},{4,1},{5,0},{6,3},{7,2},{8,13},{9,12},{10,... | collective-permute-start | bytes 663560 | tf_op jit(solution)/shard_map/ppermute | solution.py:267
  29.1 16.3 %collective-permute-start.10 = (bf16[96,1152]{1,0:T(8,128)(2,1)S(1)}, bf16[96,1152]{1,0:T(8,128)(2,1)S(1)}, u32[]{:S(2)}, u32[]{:S(2)}) collective-permute-start(bf16[96,1152]{1,0:T(8,128)(2,1)S(1)} %get-tuple-element.33), channel_id=1, source_target_pairs={{0,5},{1,4},{2,7},{3,6},{4,1},{5,0},{6,3},{7,2},{8,13},{9,12},{10,... | collective-permute-start | bytes 663560 | tf_op jit(solution)/shard_map/ppermute | solution.py:267
  30.5 19.2 %collective-permute-start.8 = (bf16[96,1152]{1,0:T(8,128)(2,1)S(1)}, bf16[96,1152]{1,0:T(8,128)(2,1)S(1)}, u32[]{:S(2)}, u32[]{:S(2)}) collective-permute-start(bf16[96,1152]{1,0:T(8,128)(2,1)S(1)} %get-tuple-element.32), channel_id=1, source_target_pairs={{0,1},{1,0},{2,3},{3,2},{4,5},{5,4},{6,7},{7,6},{8,9},{9,8},{10,11... | collective-permute-start | bytes 663560 | tf_op jit(solution)/shard_map/ppermute | solution.py:267
  32.6 17.2 %collective-permute-start.9 = (bf16[96,1152]{1,0:T(8,128)(2,1)S(1)}, bf16[96,1152]{1,0:T(8,128)(2,1)S(1)}, u32[]{:S(2)}, u32[]{:S(2)}) collective-permute-start(bf16[96,1152]{1,0:T(8,128)(2,1)S(1)} %get-tuple-element.34), channel_id=1, source_target_pairs={{0,4},{1,5},{2,6},{3,7},{4,0},{5,1},{6,2},{7,3},{8,12},{9,13},{10,... | collective-permute-start | bytes 663560 | tf_op jit(solution)/shard_map/ppermute | solution.py:267
  45.2 6.4 %collective-permute-start.4 = (bf16[96,384]{1,0:T(8,128)(2,1)S(1)}, bf16[96,384]{1,0:T(8,128)(2,1)S(1)}, u32[]{:S(2)}, u32[]{:S(2)}) collective-permute-start(bf16[96,384]{1,0:T(8,128)(2,1)S(1)} %get-tuple-element.35), channel_id=1, source_target_pairs={{0,8},{8,0},{16,24},{24,16},{1,9},{9,1},{17,25},{25,17},{2,10},{10... | collective-permute-start | bytes 221192 | tf_op jit(solution)/shard_map/ppermute | solution.py:274
  45.3 10.1 %collective-permute-start.5 = (bf16[96,384]{1,0:T(8,128)(2,1)S(1)}, bf16[96,384]{1,0:T(8,128)(2,1)S(1)}, u32[]{:S(2)}, u32[]{:S(2)}) collective-permute-start(bf16[96,384]{1,0:T(8,128)(2,1)S(1)} %get-tuple-element.36), channel_id=1, source_target_pairs={{0,16},{8,24},{16,0},{24,8},{1,17},{9,25},{17,1},{25,9},{2,18},{10... | collective-permute-start | bytes 221192 | tf_op jit(solution)/shard_map/ppermute | solution.py:274
  45.4 10.0 %collective-permute-start.6 = (bf16[96,384]{1,0:T(8,128)(2,1)S(1)}, bf16[96,384]{1,0:T(8,128)(2,1)S(1)}, u32[]{:S(2)}, u32[]{:S(2)}) collective-permute-start(bf16[96,384]{1,0:T(8,128)(2,1)S(1)} %select_convert_fusion.3), channel_id=1, source_target_pairs={{0,24},{8,16},{16,8},{24,0},{1,25},{9,17},{17,9},{25,1},{2,26},{10... | collective-permute-start | bytes 221192 | tf_op jit(solution)/shard_map/ppermute | solution.py:274
  50.9 5.7 %collective-permute-start.11 = (bf16[96,384]{1,0:T(8,128)(2,1)S(1)}, bf16[96,384]{1,0:T(8,128)(2,1)S(1)}, u32[]{:S(2)}, u32[]{:S(2)}) collective-permute-start(bf16[96,384]{1,0:T(8,128)(2,1)S(1)} %get-tuple-element.37), channel_id=1, source_target_pairs={{0,8},{8,0},{16,24},{24,16},{1,9},{9,1},{17,25},{25,17},{2,10},{10... | collective-permute-start | bytes 221192 | tf_op jit(solution)/shard_map/ppermute | solution.py:274
  51.0 8.2 %collective-permute-start.12 = (bf16[96,384]{1,0:T(8,128)(2,1)S(1)}, bf16[96,384]{1,0:T(8,128)(2,1)S(1)}, u32[]{:S(2)}, u32[]{:S(2)}) collective-permute-start(bf16[96,384]{1,0:T(8,128)(2,1)S(1)} %get-tuple-element.38), channel_id=1, source_target_pairs={{0,16},{8,24},{16,0},{24,8},{1,17},{9,25},{17,1},{25,9},{2,18},{10... | collective-permute-start | bytes 221192 | tf_op jit(solution)/shard_map/ppermute | solution.py:274
  51.6 7.6 %collective-permute-start.13 = (bf16[96,384]{1,0:T(8,128)(2,1)S(1)}, bf16[96,384]{1,0:T(8,128)(2,1)S(1)}, u32[]{:S(2)}, u32[]{:S(2)}) collective-permute-start(bf16[96,384]{1,0:T(8,128)(2,1)S(1)} %select_convert_fusion), channel_id=1, source_target_pairs={{0,24},{8,16},{16,8},{24,0},{1,25},{9,17},{17,9},{25,1},{2,26},{10... | collective-permute-start | bytes 221192 | tf_op jit(solution)/shard_map/ppermute | solution.py:274

commit v2 on v1

--- a/solution.py
+++ b/solution.py
@@ -12,6 +12,7 @@
 GRAIN = 16
 STEP = 2
 GRANT = 48 * 2**20
+SMALL = 4 * 2**20
 PARTS = (1, 1)
 
 
@@ -21,45 +22,62 @@
     return tuple(p_own // sum(PARTS) * part for part in PARTS)
 
 
-def blocks_of(dims, chunk):
-    general, _, gen_size, act_size = dims
-    parts = parts_of(general // gen_size)
-    p_from = sum(parts[:chunk])
-    return [
-        (g, a, p_from, p_from + parts[chunk])
-        for parity in (1, 0)
-        for g in range(parity, gen_size, 2)
-        for a in range(act_size)
-    ]
+STAGES = (
+    ("x", ((0, 1, 0), (1, 1, 0))),
+    ("y", ((1, 0, 1), (1, 1, 1))),
+    ("xy", ((1, 0, 0),)),
+    ("yx", ((0, 1, 1),)),
+    ("re", ((0, 0, 0),)),
+    ("im", ((0, 0, 1),)),
+)
+
+
+def rows_of_stages(dims, chunk):
+    general, active, gen_size, act_size = dims
+    size = parts_of(general // gen_size)[chunk] * (active // act_size)
+    found, row = {}, 0
+    for name, members in STAGES:
+        found[name] = (row, row + size * len(members))
+        row += size * len(members)
+    return found, row
 
 
 def make_weights(dims, chunk, t, column, bra_pack, ket_pack, weights):
     general, active, gen_size, act_size = dims
     p_own, u_own = general // gen_size, active // act_size
+    parts = parts_of(p_own)
+    p_from = sum(parts[:chunk])
+    size = parts[chunk] * u_own
+    order = [member for _, members in STAGES for member in members]
     me_gen, me_act = lax.axis_index("gen"), lax.axis_index("act")
     left, right = slice(column, column + LANES), slice(column + LANES, column + 2 * LANES)
-    row = 0
-    for g, a, p_from, p_to in blocks_of(dims, chunk):
-        p_first = (me_gen ^ g) * p_own
-        u_first = pl.multiple_of((me_act ^ a) * u_own, 8)
-        ket_re = ket_pack[t, pl.ds(u_first, u_own), :]
-        ket_im = ket_pack[t, pl.ds(active + u_first, u_own), :]
-        real, imag = [], []
-        for p in range(p_from, p_to):
-            bra_re = bra_pack[t, pl.ds(p_first + p, 1), :]
-            bra_im = bra_pack[t, pl.ds(general + p_first + p, 1), :]
-            real.append(bra_re * ket_re + bra_im * ket_im)
-            imag.append(bra_re * ket_im - bra_im * ket_re)
-        rows = 2 * (p_to - p_from) * u_own
-        first = jnp.concatenate(real + imag, axis=0).astype(jnp.bfloat16)
-        second = jnp.concatenate([-x for x in imag] + real, axis=0).astype(jnp.bfloat16)
-        weights[row : row + rows, left] = first
-        weights[row : row + rows, right] = second
-        row += rows
+    for core in (1, 0):
+        for q in range(gen_size // 2):
+            for a in range(act_size):
+                p_first = (me_gen ^ (2 * q + core)) * p_own + p_from
+                u_first = pl.multiple_of((me_act ^ a) * u_own, 8)
+                ket_re = ket_pack[t, pl.ds(u_first, u_own), :]
+                ket_im = ket_pack[t, pl.ds(active + u_first, u_own), :]
+                real, imag = [], []
+                for p in range(parts[chunk]):
+                    bra_re = bra_pack[t, pl.ds(p_first + p, 1), :]
+                    bra_im = bra_pack[t, pl.ds(general + p_first + p, 1), :]
+                    real.append(bra_re * ket_re + bra_im * ket_im)
+                    imag.append(bra_re * ket_im - bra_im * ket_re)
+                real = jnp.concatenate(real, axis=0)
+                imag = jnp.concatenate(imag, axis=0)
+                real_low = real.astype(jnp.bfloat16)
+                base = (1 - core) * len(order) * size
+                row = base + order.index((q, a, 0)) * size
+                weights[row : row + size, left] = real_low
+                weights[row : row + size, right] = (-imag).astype(jnp.bfloat16)
+                row = base + order.index((q, a, 1)) * size
+                weights[row : row + size, left] = imag.astype(jnp.bfloat16)
+                weights[row : row + size, right] = real_low
 
 
 def product_kernel(dims, chunk, blocks, width, counts_ref, *refs):
-    outs = 1 + len(blocks_of(dims, chunk)) // 2
+    outs = 1 + len(STAGES)
     if chunk == 0:
         rows_ref, ints_ref = refs[:2]
         results = refs[2 : 2 + outs]
@@ -173,15 +191,15 @@
 
 
 def products(dims, chunk, counts, operands, integrals):
-    general, active, _, act_size = dims
+    general, active, _, _ = dims
     blocks, _, width, columns = integrals.shape
-    u_own = active // act_size
     tiles = -(-blocks * width // (STEP * LANES)) * STEP
-    sizes = [2 * (p_to - p_from) * u_own for _, _, p_from, p_to in blocks_of(dims, chunk)]
-    rows = sum(sizes)
-    outs = [jax.ShapeDtypeStruct((rows // 2, columns), jnp.bfloat16)]
+    ranges, half = rows_of_stages(dims, chunk)
+    rows = 2 * half
+    outs = [jax.ShapeDtypeStruct((half, columns), jnp.bfloat16)]
     outs += [
-        jax.ShapeDtypeStruct((size, columns), jnp.float32) for size in sizes[len(sizes) // 2 :]
+        jax.ShapeDtypeStruct((last - first, columns), jnp.float32)
+        for first, last in ranges.values()
     ]
     if chunk == 0:
         outs += [
@@ -217,11 +235,93 @@
     return own, width, [min(s, columns - width) for s in starts]
 
 
-def choose(index, values):
-    result = values[0]
-    for i in range(1, len(values)):
-        result = jnp.where(index == i, values[i], result)
-    return result
+def small(kernel, outs, *operands):
+    return pl.pallas_call(
+        kernel,
+        out_shape=outs,
+        in_specs=[VMEM] * len(operands),
+        out_specs=jax.tree.map(lambda _: VMEM, outs),
+        compiler_params=pltpu.CompilerParams(vmem_limit_bytes=SMALL),
+        cost_estimate=pl.CostEstimate(
+            flops=sum(x.size for x in operands),
+            bytes_accessed=4 * sum(x.size for x in operands),
+            transcendentals=0,
+        ),
+    )(*operands)
+
+
+def total_call(kernel, outs, shape, *operands):
+    scratch = [pltpu.VMEM(shape, jnp.float32)] if outs else []
+    outs = outs or [jax.ShapeDtypeStruct(shape, jnp.float32)]
+    return pl.pallas_call(
+        kernel,
+        out_shape=outs,
+        in_specs=[VMEM] * len(operands),
+        out_specs=[VMEM] * len(outs),
+        scratch_shapes=scratch,
+        compiler_params=pltpu.CompilerParams(vmem_limit_bytes=SMALL),
+        cost_estimate=pl.CostEstimate(
+            flops=sum(x.size for x in operands),
+            bytes_accessed=4 * sum(x.size for x in operands),
+            transcendentals=0,
+        ),
+    )(*operands)
+
+
+def wide(ref, ranges, name):
+    first, last = ranges[name]
+    return ref[first:last].astype(jnp.float32)
+
+
+def first_kernel(ranges, x_ref, y_ref, got_ref, x_out, y_out):
+    x_out[...] = (x_ref[...] + wide(got_ref, ranges, "x")).astype(x_out.dtype)
+    y_out[...] = (y_ref[...] + wide(got_ref, ranges, "y")).astype(y_out.dtype)
+
+
+def second_kernel(ranges, xy_ref, yx_ref, got_ref, from_x, from_y, xy_out, yx_out):
+    size = xy_ref.shape[0]
+    for kept, name, arrived, out in (
+        (xy_ref, "xy", from_x, xy_out), (yx_ref, "yx", from_y, yx_out)
+    ):
+        value = kept[...] + wide(got_ref, ranges, name) + arrived[size:].astype(jnp.float32)
+        out[...] = value.astype(out.dtype)
+
+
+def total_kernel(ranges, parts, re_ref, im_ref, got_ref, from_x, from_y, from_xy, from_yx, *outs):
+    size = re_ref.shape[0]
+    total = outs[-1]
+    for row, kept, name, first, second in (
+        (0, re_ref, "re", from_x, from_xy), (size, im_ref, "im", from_y, from_yx)
+    ):
+        value = kept[...] + wide(got_ref, ranges, name) + first[:size].astype(jnp.float32)
+        total[row : row + size] = value + second[...].astype(jnp.float32)
+    if parts:
+        columns = total.shape[1]
+        own, width, _ = window_of(columns, parts)
+        me = lax.axis_index("ao")
+        for k, out in enumerate(outs[:-1]):
+            first = jnp.minimum((me ^ k) * own // LANES * LANES, columns - width)
+            cut = total[:, pl.ds(pl.multiple_of(first, LANES), width)]
+            out[...] = cut.astype(out.dtype)
+
+
+def final_kernel(parts, columns, *refs):
+    out_ref = refs[-1]
+    own, width, _ = window_of(columns, parts)
+    me = lax.axis_index("ao")
+    first = jnp.minimum(me * own // LANES * LANES, columns - width)
+    shift = me * own - first
+    p_from = 0
+    for j in range(len(refs) // parts):
+        group = refs[j * parts : (j + 1) * parts]
+        value = group[0][...]
+        for ref in group[1:]:
+            value = value + ref[...].astype(jnp.float32)
+        value = pltpu.roll(value, jnp.where(shift == 0, 0, width - shift), 1)[:, :own]
+        u_own = out_ref.shape[2]
+        part = value.shape[0] // (2 * u_own)
+        out_ref[:, p_from : p_from + part] = value.reshape(2, part, u_own, own)
+        p_from += part
 
 
 def swap(size, bit):
@@ -234,57 +334,63 @@
     ao_size = lax.axis_size("ao")
     gen_size = lax.axis_size("gen")
     act_size = lax.axis_size("act")
-    me_ao = lax.axis_index("ao")
     bra = jnp.swapaxes(bra_rows, 2, 3)
     ket = jnp.swapaxes(ket_rows, 2, 3)
     p_own, u_own = general // gen_size, active // act_size
     dims = (general, active, gen_size, act_size)
     counts = jnp.concatenate([pair_count, block_count])
     operands = (jnp.concatenate([bra, ket], axis=2),)
-    own, width, starts = window_of(columns, ao_size)
+    own, width, _ = window_of(columns, ao_size)
     outs = []
-    kept = gen_size // 2 * act_size
+    assert (gen_size, act_size) == (4, 2)
     for chunk, part in enumerate(parts_of(p_own)):
         block = 2 * part * u_own
+        ranges, _ = rows_of_stages(dims, chunk)
         send, *keep = products(dims, chunk, counts, operands, integrals)
         if chunk == 0:
-            operands = tuple(keep[kept:])
+            operands = tuple(keep[len(ranges) :])
         got = lax.ppermute(send, "gen", swap(gen_size, 1))
-        index = 0
-        for g in range(0, gen_size, 2):
-            for a in range(act_size):
-                piece = keep[index] + got[index * block : (index + 1) * block].astype(jnp.float32)
-                index += 1
-                if g == 0 and a == 0:
-                    total = piece
-                    continue
-                pairs = [
-                    (i * act_size + k, (i ^ g) * act_size + (k ^ a))
-                    for i in range(gen_size)
-                    for k in range(act_size)
-                ]
-                low = piece.astype(jnp.bfloat16)
-                arrived = lax.ppermute(low, ("gen", "act"), pairs)
-                total = total + arrived.astype(jnp.float32)
-        if ao_size <= 4:
-            windows = [total[:, s : s + width] for s in starts]
-            value = choose(me_ao, windows)
-            for k in range(1, ao_size):
-                cut = choose(me_ao ^ k, windows).astype(jnp.bfloat16)
-                arrived = lax.ppermute(cut, "ao", swap(ao_size, k))
-                value = value + arrived.astype(jnp.float32)
-            shifts = [own * a - starts[a] for a in range(ao_size)]
-            value = choose(me_ao, [value[:, s : s + own] for s in shifts])
+        keep = dict(zip(ranges, keep))
+
+        def move(value, axis, bit):
+            return lax.ppermute(value, axis, swap(lax.axis_size(axis), bit))
+
+        low = jax.ShapeDtypeStruct(keep["x"].shape, jnp.bfloat16)
+        to_x, to_y = small(
+            functools.partial(first_kernel, ranges), [low, low],
+            keep["x"], keep["y"], got,
+        )
+        from_x, from_y = move(to_x, "act", 1), move(to_y, "gen", 2)
+        low = jax.ShapeDtypeStruct(keep["xy"].shape, jnp.bfloat16)
+        to_xy, to_yx = small(
+            functools.partial(second_kernel, ranges), [low, low],
+            keep["xy"], keep["yx"], got, from_x, from_y,
+        )
+        from_xy, from_yx = move(to_xy, "gen", 2), move(to_yx, "act", 1)
+        parts = ao_size if ao_size <= 4 else 0
+        if parts:
+            totals = [
+                jax.ShapeDtypeStruct((block, width), jnp.bfloat16 if k else jnp.float32)
+                for k in range(parts)
+            ]
         else:
-            total = total.reshape(block, ao_size, own)
+            totals = []
+        windows = total_call(
+            functools.partial(total_kernel, ranges, parts), totals,
+            (block, columns), keep["re"], keep["im"], got, from_x, from_y, from_xy, from_yx,
+        )
+        if parts:
+            outs.append(windows[0])
+            outs += [move(windows[k], "ao", k) for k in range(1, parts)]
+        else:
+            total = windows[0].reshape(block, ao_size, own)
             total = jnp.swapaxes(total, 0, 1).reshape(ao_size * block, own)
             value = lax.psum_scatter(total, "ao", scatter_dimension=0, tiled=True)
-        outs.append(value.reshape(2, part, u_own, own))
+            outs.append(value.reshape(2, part, u_own, own))
+    if parts:
+        result = jax.ShapeDtypeStruct((2, p_own, u_own, own), jnp.float32)
+        return small(functools.partial(final_kernel, parts, columns), result, *outs)
     return jnp.concatenate(outs, axis=1)
-
-
-def swap(size, bit):
-    return [(i, i ^ bit) for i in range(size)]
 
 
 def solution(mesh):

time: 60.5 us -> 54.1 us (0.89)
  other arithmetic: 7.75 us -> 1.75 us
  starting transfers between devices: 24.5 us -> 23.5 us
  waiting for transfers between devices: 16.4 us -> 17.4 us
    convert_element_type x6 -> x0, other arithmetic: 2.68 us -> none  [the longest x2 2.53 us: local(): low = piece.astype(jnp.bfloat16)]
    add x4 -> x0, other arithmetic: 2.23 us -> none  [the longest x2 2.12 us: local(): total = total + arrived.astype(jnp.float32)]
    pallas_call x2, Pallas kernels: 10.7 us -> 8.99 us  [products(): pl.pallas_call(functools.partial(product_kernel, dims, chunk, blocks, wid...]
    pallas_call x0 -> x7, Pallas kernels: none -> 1.55 us  [the longest x5 1.23 us: small(): pl.pallas_call(kernel, out_shape=outs, in_specs=[VMEM] * len(operands), o...]
    ppermute x12 -> x14, starting transfers between devices: 20.9 us -> 19.8 us  [move(): return lax.ppermute(value, axis, swap(lax.axis_size(axis), bit))]
    ppermute x12 -> x14, waiting for transfers between devices: 16.4 us -> 17.4 us  [move(): return lax.ppermute(value, axis, swap(lax.axis_size(axis), bit))]
    concatenate x1 -> x0, other arithmetic: 0.73 us -> none  [local(): return jnp.concatenate(outs, axis=1)]
  transfers between devices with their start and end apart: 14 -> 16, of which waited for: 4 -> 8; matrix products, arithmetic and copies ran while one was open for 8% -> 0% of each run, Pallas kernels for 9% -> 10%
where the time goes in v2:
time: 54.1 us; the launch traced here: 53.9 us
  starting transfers between devices  23.5 us (43%)
  waiting for transfers between devices  17.4 us (32%)
  Pallas kernels  10.5 us (19%)
  other arithmetic  1.75 us (3%)
  between operations  0.75 us (1%)
    ppermute x14, starting transfers between devices, move(): return lax.ppermute(value, axis, swap(lax.axis_size(axis), bit))  19.8 us
    ppermute x14, waiting for transfers between devices, move(): return lax.ppermute(value, axis, swap(lax.axis_size(axis), bit))  17.4 us
    pallas_call x2, Pallas kernels, products(): pl.pallas_call(functools.partial(product_kernel, dims, chunk, blocks, wid...  8.99 us
    ppermute x2, starting transfers between devices, local(): got = lax.ppermute(send, 'gen', swap(gen_size, 1))  3.71 us
    pallas_call x5, Pallas kernels, small(): pl.pallas_call(kernel, out_shape=outs, in_specs=[VMEM] * len(operands), o...  1.23 us
  transfers between devices with their start and end apart: 16, of which 8 were waited for; matrix products, arithmetic and copies ran while one was open for 0% of the time, Pallas kernels for 10%

profile of v2, /device:TPU:0, one launch (start us, length us, event | category | flops | bytes accessed | tf_op | source)
XLA Modules:
  0.0 53.9 jit_solution(1843282046055966706)
XLA Ops:
  0.7 0.7 %pad_add_fusion.counts_ref = s32[13]{0:T(128)S(1)} fusion(s32[1]{0:T(128)S(6)} %copy.6, s32[12]{0:T(128)} %param.9), kind=kLoop, calls=%fused_computation.1 | loop fusion | flops 13 | bytes 104 | tf_op jit(solution)/shard_map/concatenate | solution.py:341
  1.4 1.0 %pad_maximum_fusion.refs_0_ = bf16[12,2,64,128]{3,2,1,0:T(8,128)(2,1)S(1)} fusion(bf16[12,2,48,128]{3,2,1,0:T(8,128)(2,1)} %bitcast.2, bf16[12,2,16,128]{3,2,1,0:T(8,128)(2,1)} %bitcast.3), kind=kLoop, calls=%fused_computation | loop fusion | flops 786432 | bytes 786432 | tf_op jit(solution)/shard_map/concatenate | solution.py:342
  2.4 4.5 %shard_map.55 = (bf16[384,1152]{1,0:T(8,128)(2,1)S(1)}, f32[96,1152]{1,0:T(8,128)S(1)}, f32[96,1152]{1,0:T(8,128)S(1)}, f32[48,1152]{1,0:T(8,128)S(1)}, f32[48,1...) custom-call(s32[13]{0:T(128)S(1)} %pad_add_fusion.counts_ref, ...), custom_call_target="tpu_custom_call" | custom-call | flops 2717908992 | bytes 2654208 | tf_op jit(solution)/shard_map/pallas_call | solution.py:209
  6.9 2.1 %collective-permute-start = (bf16[384,1152]{1,0:T(8,128)(2,1)S(1)}, bf16[384,1152]{1,0:T(8,128)(2,1)S(1)}, u32[]{:S(2)}, u32[]{:S(2)}) collective-permute-start(bf16[384,1152]{1,0:T(8,128)(2,1)S(1)} %get-tuple-element.39), channel_id=1, source_target_pairs={{0,2},{2,0},{4,6},{6,4},{1,3},{3,1},{5,7},{7,5},{8,10},{10,8},{12,... | collective-permute-start | bytes 2654216 | tf_op jit(solution)/shard_map/ppermute | solution.py:352
  9.0 4.5 %shard_map.59 = (bf16[384,1152]{1,0:T(8,128)(2,1)S(1)}, f32[96,1152]{1,0:T(8,128)S(1)}, f32[96,1152]{1,0:T(8,128)S(1)}, f32[48,1152]{1,0:T(8,128)S(1)}, f32[48,1...) custom-call(s32[13]{0:T(128)S(1)} %pad_add_fusion.counts_ref, ...), custom_call_target="tpu_custom_call" | custom-call | flops 2717908992 | bytes 2654208 | tf_op jit(solution)/shard_map/pallas_call | solution.py:209
  13.5 1.6 %collective-permute-start.8 = (bf16[384,1152]{1,0:T(8,128)(2,1)S(1)}, bf16[384,1152]{1,0:T(8,128)(2,1)S(1)}, u32[]{:S(2)}, u32[]{:S(2)}) collective-permute-start(bf16[384,1152]{1,0:T(8,128)(2,1)S(1)} %get-tuple-element.56), channel_id=1, source_target_pairs={{0,2},{2,0},{4,6},{6,4},{1,3},{3,1},{5,7},{7,5},{8,10},{10,8},{12,... | collective-permute-start | bytes 2654216 | tf_op jit(solution)/shard_map/ppermute | solution.py:352
  15.1 0.1 shard_map.56
  15.2 8.2 %collective-permute-start.1 = (bf16[96,1152]{1,0:T(8,128)(2,1)S(1)}, bf16[96,1152]{1,0:T(8,128)(2,1)S(1)}, u32[]{:S(2)}, u32[]{:S(2)}) collective-permute-start(bf16[96,1152]{1,0:T(8,128)(2,1)S(1)} %get-tuple-element.42), channel_id=1, source_target_pairs={{0,1},{1,0},{2,3},{3,2},{4,5},{5,4},{6,7},{7,6},{8,9},{9,8},{10,11... | collective-permute-start | bytes 663560 | tf_op jit(solution)/shard_map/ppermute | solution.py:356
  23.4 0.1 shard_map.60
  23.5 2.3 %collective-permute-start.9 = (bf16[96,1152]{1,0:T(8,128)(2,1)S(1)}, bf16[96,1152]{1,0:T(8,128)(2,1)S(1)}, u32[]{:S(2)}, u32[]{:S(2)}) collective-permute-start(bf16[96,1152]{1,0:T(8,128)(2,1)S(1)} %get-tuple-element.59), channel_id=1, source_target_pairs={{0,1},{1,0},{2,3},{3,2},{4,5},{5,4},{6,7},{7,6},{8,9},{9,8},{10,11... | collective-permute-start | bytes 663560 | tf_op jit(solution)/shard_map/ppermute | solution.py:356
  25.8 3.9 %collective-permute-done.1.from_x = bf16[96,1152]{1,0:T(8,128)(2,1)S(1)} collective-permute-done((bf16[96,1152]{1,0:T(8,128)(2,1)S(1)}, bf16[96,1152]{1,0:T(8,128)(2,1)S(1)}, u32[]{:S(2)}, u32[]{:S(2)}) %collective-permute-start.1) | collective-permute-done | bytes 221216 | tf_op jit(solution)/shard_map/ppermute | solution.py:356
  29.6 2.0 %collective-permute-done.2.from_y = bf16[96,1152]{1,0:T(8,128)(2,1)S(1)} collective-permute-done((bf16[96,1152]{1,0:T(8,128)(2,1)S(1)}, bf16[96,1152]{1,0:T(8,128)(2,1)S(1)}, u32[]{:S(2)}, u32[]{:S(2)}) %collective-permute-start.2) | collective-permute-done | bytes 221216 | tf_op jit(solution)/shard_map/ppermute | solution.py:356
  31.7 0.1 shard_map.57
  31.7 0.1 collective-permute-start.3
  31.8 0.1 collective-permute-start.4
  32.0 2.4 %collective-permute-done.9.from_x = bf16[96,1152]{1,0:T(8,128)(2,1)S(1)} collective-permute-done((bf16[96,1152]{1,0:T(8,128)(2,1)S(1)}, bf16[96,1152]{1,0:T(8,128)(2,1)S(1)}, u32[]{:S(2)}, u32[]{:S(2)}) %collective-permute-start.9) | collective-permute-done | bytes 221216 | tf_op jit(solution)/shard_map/ppermute | solution.py:356
  34.4 2.0 %collective-permute-done.10.from_y = bf16[96,1152]{1,0:T(8,128)(2,1)S(1)} collective-permute-done((bf16[96,1152]{1,0:T(8,128)(2,1)S(1)}, bf16[96,1152]{1,0:T(8,128)(2,1)S(1)}, u32[]{:S(2)}, u32[]{:S(2)}) %collective-permute-start.10) | collective-permute-done | bytes 221216 | tf_op jit(solution)/shard_map/ppermute | solution.py:356
  36.4 0.1 shard_map.61
  36.5 0.1 collective-permute-start.11
  36.6 0.1 collective-permute-start.12
  36.7 1.6 %collective-permute-done.3.from_xy = bf16[48,1152]{1,0:T(8,128)(2,1)S(1)} collective-permute-done((bf16[48,1152]{1,0:T(8,128)(2,1)S(1)}, bf16[48,1152]{1,0:T(8,128)(2,1)S(1)}, u32[]{:S(2)}, u32[]{:S(2)}) %collective-permute-start.3) | collective-permute-done | bytes 110624 | tf_op jit(solution)/shard_map/ppermute | solution.py:356
  38.3 0.2 shard_map.58
  38.4 0.1 collective-permute-start.5
  38.5 0.1 collective-permute-start.6
  38.6 4.3 %collective-permute-start.7 = (bf16[96,384]{1,0:T(8,128)(2,1)S(1)}, bf16[96,384]{1,0:T(8,128)(2,1)S(1)}, u32[]{:S(2)}, u32[]{:S(2)}) collective-permute-start(bf16[96,384]{1,0:T(8,128)(2,1)S(1)} %get-tuple-element.51), channel_id=1, source_target_pairs={{0,24},{8,16},{16,8},{24,0},{1,25},{9,17},{17,9},{25,1},{2,26},{10... | collective-permute-start | bytes 221192 | tf_op jit(solution)/shard_map/ppermute | solution.py:356
  42.9 0.2 shard_map.62
  43.1 0.6 %collective-permute-start.14 = (bf16[96,384]{1,0:T(8,128)(2,1)S(1)}, bf16[96,384]{1,0:T(8,128)(2,1)S(1)}, u32[]{:S(2)}, u32[]{:S(2)}) collective-permute-start(bf16[96,384]{1,0:T(8,128)(2,1)S(1)} %get-tuple-element.67), channel_id=1, source_target_pairs={{0,16},{8,24},{16,0},{24,8},{1,17},{9,25},{17,1},{25,9},{2,18},{10... | collective-permute-start | bytes 221192 | tf_op jit(solution)/shard_map/ppermute | solution.py:356
  43.7 3.8 %collective-permute-start.15 = (bf16[96,384]{1,0:T(8,128)(2,1)S(1)}, bf16[96,384]{1,0:T(8,128)(2,1)S(1)}, u32[]{:S(2)}, u32[]{:S(2)}) collective-permute-start(bf16[96,384]{1,0:T(8,128)(2,1)S(1)} %get-tuple-element.68), channel_id=1, source_target_pairs={{0,24},{8,16},{16,8},{24,0},{1,25},{9,17},{17,9},{25,1},{2,26},{10... | collective-permute-start | bytes 221192 | tf_op jit(solution)/shard_map/ppermute | solution.py:356
  47.5 1.2 %collective-permute-done.6.refs_2_ = bf16[96,384]{1,0:T(8,128)(2,1)S(1)} collective-permute-done((bf16[96,384]{1,0:T(8,128)(2,1)S(1)}, bf16[96,384]{1,0:T(8,128)(2,1)S(1)}, u32[]{:S(2)}, u32[]{:S(2)}) %collective-permute-start.6) | collective-permute-done | bytes 73760 | tf_op jit(solution)/shard_map/ppermute | solution.py:356
  48.7 0.5 collective-permute-done.13.refs_5_
  49.2 3.8 %collective-permute-done.14.refs_6_ = bf16[96,384]{1,0:T(8,128)(2,1)S(1)} collective-permute-done((bf16[96,384]{1,0:T(8,128)(2,1)S(1)}, bf16[96,384]{1,0:T(8,128)(2,1)S(1)}, u32[]{:S(2)}, u32[]{:S(2)}) %collective-permute-start.14) | collective-permute-done | bytes 73760 | tf_op jit(solution)/shard_map/ppermute | solution.py:356
  53.0 0.9 %shard_map.63 = f32[2,4,24,288]{3,2,1,0:T(8,128)} custom-call(f32[96,384]{1,0:T(8,128)S(1)} %get-tuple-element.48.refs_0_, bf16[96,384]{1,0:T(8,128)(2,1)S(1)} %collective-permute-done.5.refs_1_, bf16[96,384]{1,0:T(8,128)(2,1)S(1)} %collective-permute-done.6.refs_2_, bf16[96,384]{1,0:T(8,128)(2,1)S(1)} %collective-permute-done.7.refs_3_, ...), custom_call_target="tpu_custom_call" | custom-call | flops 294912 | bytes 1179648 | tf_op jit(solution)/shard_map/pallas_call | solution.py:239
  (11 shorter events, 0.1 us)
Async XLA Ops:
  6.9 8.2 %collective-permute-start = (bf16[384,1152]{1,0:T(8,128)(2,1)S(1)}, bf16[384,1152]{1,0:T(8,128)(2,1)S(1)}, u32[]{:S(2)}, u32[]{:S(2)}) collective-permute-start(bf16[384,1152]{1,0:T(8,128)(2,1)S(1)} %get-tuple-element.39), channel_id=1, source_target_pairs={{0,2},{2,0},{4,6},{6,4},{1,3},{3,1},{5,7},{7,5},{8,10},{10,8},{12,... | collective-permute-start | bytes 2654216 | tf_op jit(solution)/shard_map/ppermute | solution.py:352
  13.5 9.9 %collective-permute-start.8 = (bf16[384,1152]{1,0:T(8,128)(2,1)S(1)}, bf16[384,1152]{1,0:T(8,128)(2,1)S(1)}, u32[]{:S(2)}, u32[]{:S(2)}) collective-permute-start(bf16[384,1152]{1,0:T(8,128)(2,1)S(1)} %get-tuple-element.56), channel_id=1, source_target_pairs={{0,2},{2,0},{4,6},{6,4},{1,3},{3,1},{5,7},{7,5},{8,10},{10,8},{12,... | collective-permute-start | bytes 2654216 | tf_op jit(solution)/shard_map/ppermute | solution.py:352
  15.2 14.4 %collective-permute-start.1 = (bf16[96,1152]{1,0:T(8,128)(2,1)S(1)}, bf16[96,1152]{1,0:T(8,128)(2,1)S(1)}, u32[]{:S(2)}, u32[]{:S(2)}) collective-permute-start(bf16[96,1152]{1,0:T(8,128)(2,1)S(1)} %get-tuple-element.42), channel_id=1, source_target_pairs={{0,1},{1,0},{2,3},{3,2},{4,5},{5,4},{6,7},{7,6},{8,9},{9,8},{10,11... | collective-permute-start | bytes 663560 | tf_op jit(solution)/shard_map/ppermute | solution.py:356
  23.4 8.3 %collective-permute-start.2 = (bf16[96,1152]{1,0:T(8,128)(2,1)S(1)}, bf16[96,1152]{1,0:T(8,128)(2,1)S(1)}, u32[]{:S(2)}, u32[]{:S(2)}) collective-permute-start(bf16[96,1152]{1,0:T(8,128)(2,1)S(1)} %get-tuple-element.43), channel_id=1, source_target_pairs={{0,4},{2,6},{4,0},{6,2},{1,5},{3,7},{5,1},{7,3},{8,12},{10,14},{12... | collective-permute-start | bytes 663560 | tf_op jit(solution)/shard_map/ppermute | solution.py:356
  23.5 10.9 %collective-permute-start.9 = (bf16[96,1152]{1,0:T(8,128)(2,1)S(1)}, bf16[96,1152]{1,0:T(8,128)(2,1)S(1)}, u32[]{:S(2)}, u32[]{:S(2)}) collective-permute-start(bf16[96,1152]{1,0:T(8,128)(2,1)S(1)} %get-tuple-element.59), channel_id=1, source_target_pairs={{0,1},{1,0},{2,3},{3,2},{4,5},{5,4},{6,7},{7,6},{8,9},{9,8},{10,11... | collective-permute-start | bytes 663560 | tf_op jit(solution)/shard_map/ppermute | solution.py:356
  25.8 10.6 %collective-permute-start.10 = (bf16[96,1152]{1,0:T(8,128)(2,1)S(1)}, bf16[96,1152]{1,0:T(8,128)(2,1)S(1)}, u32[]{:S(2)}, u32[]{:S(2)}) collective-permute-start(bf16[96,1152]{1,0:T(8,128)(2,1)S(1)} %get-tuple-element.60), channel_id=1, source_target_pairs={{0,4},{2,6},{4,0},{6,2},{1,5},{3,7},{5,1},{7,3},{8,12},{10,14},{12... | collective-permute-start | bytes 663560 | tf_op jit(solution)/shard_map/ppermute | solution.py:356
  31.7 6.5 %collective-permute-start.3 = (bf16[48,1152]{1,0:T(8,128)(2,1)S(1)}, bf16[48,1152]{1,0:T(8,128)(2,1)S(1)}, u32[]{:S(2)}, u32[]{:S(2)}) collective-permute-start(bf16[48,1152]{1,0:T(8,128)(2,1)S(1)} %get-tuple-element.46), channel_id=1, source_target_pairs={{0,4},{2,6},{4,0},{6,2},{1,5},{3,7},{5,1},{7,3},{8,12},{10,14},{12... | collective-permute-start | bytes 331784 | tf_op jit(solution)/shard_map/ppermute | solution.py:356
  31.8 6.5 %collective-permute-start.4 = (bf16[48,1152]{1,0:T(8,128)(2,1)S(1)}, bf16[48,1152]{1,0:T(8,128)(2,1)S(1)}, u32[]{:S(2)}, u32[]{:S(2)}) collective-permute-start(bf16[48,1152]{1,0:T(8,128)(2,1)S(1)} %get-tuple-element.47), channel_id=1, source_target_pairs={{0,1},{1,0},{2,3},{3,2},{4,5},{5,4},{6,7},{7,6},{8,9},{9,8},{10,11... | collective-permute-start | bytes 331784 | tf_op jit(solution)/shard_map/ppermute | solution.py:356
  36.5 6.4 %collective-permute-start.11 = (bf16[48,1152]{1,0:T(8,128)(2,1)S(1)}, bf16[48,1152]{1,0:T(8,128)(2,1)S(1)}, u32[]{:S(2)}, u32[]{:S(2)}) collective-permute-start(bf16[48,1152]{1,0:T(8,128)(2,1)S(1)} %get-tuple-element.63), channel_id=1, source_target_pairs={{0,4},{2,6},{4,0},{6,2},{1,5},{3,7},{5,1},{7,3},{8,12},{10,14},{12... | collective-permute-start | bytes 331784 | tf_op jit(solution)/shard_map/ppermute | solution.py:356
  36.6 6.3 %collective-permute-start.12 = (bf16[48,1152]{1,0:T(8,128)(2,1)S(1)}, bf16[48,1152]{1,0:T(8,128)(2,1)S(1)}, u32[]{:S(2)}, u32[]{:S(2)}) collective-permute-start(bf16[48,1152]{1,0:T(8,128)(2,1)S(1)} %get-tuple-element.64), channel_id=1, source_target_pairs={{0,1},{1,0},{2,3},{3,2},{4,5},{5,4},{6,7},{7,6},{8,9},{9,8},{10,11... | collective-permute-start | bytes 331784 | tf_op jit(solution)/shard_map/ppermute | solution.py:356
  38.4 5.3 %collective-permute-start.5 = (bf16[96,384]{1,0:T(8,128)(2,1)S(1)}, bf16[96,384]{1,0:T(8,128)(2,1)S(1)}, u32[]{:S(2)}, u32[]{:S(2)}) collective-permute-start(bf16[96,384]{1,0:T(8,128)(2,1)S(1)} %get-tuple-element.49), channel_id=1, source_target_pairs={{0,8},{8,0},{16,24},{24,16},{1,9},{9,1},{17,25},{25,17},{2,10},{10... | collective-permute-start | bytes 221192 | tf_op jit(solution)/shard_map/ppermute | solution.py:356
  38.5 10.2 %collective-permute-start.6 = (bf16[96,384]{1,0:T(8,128)(2,1)S(1)}, bf16[96,384]{1,0:T(8,128)(2,1)S(1)}, u32[]{:S(2)}, u32[]{:S(2)}) collective-permute-start(bf16[96,384]{1,0:T(8,128)(2,1)S(1)} %get-tuple-element.50), channel_id=1, source_target_pairs={{0,16},{8,24},{16,0},{24,8},{1,17},{9,25},{17,1},{25,9},{2,18},{10... | collective-permute-start | bytes 221192 | tf_op jit(solution)/shard_map/ppermute | solution.py:356
  38.6 10.1 %collective-permute-start.7 = (bf16[96,384]{1,0:T(8,128)(2,1)S(1)}, bf16[96,384]{1,0:T(8,128)(2,1)S(1)}, u32[]{:S(2)}, u32[]{:S(2)}) collective-permute-start(bf16[96,384]{1,0:T(8,128)(2,1)S(1)} %get-tuple-element.51), channel_id=1, source_target_pairs={{0,24},{8,16},{16,8},{24,0},{1,25},{9,17},{17,9},{25,1},{2,26},{10... | collective-permute-start | bytes 221192 | tf_op jit(solution)/shard_map/ppermute | solution.py:356
  43.1 6.1 %collective-permute-start.13 = (bf16[96,384]{1,0:T(8,128)(2,1)S(1)}, bf16[96,384]{1,0:T(8,128)(2,1)S(1)}, u32[]{:S(2)}, u32[]{:S(2)}) collective-permute-start(bf16[96,384]{1,0:T(8,128)(2,1)S(1)} %get-tuple-element.66), channel_id=1, source_target_pairs={{0,8},{8,0},{16,24},{24,16},{1,9},{9,1},{17,25},{25,17},{2,10},{10... | collective-permute-start | bytes 221192 | tf_op jit(solution)/shard_map/ppermute | solution.py:356
  43.1 9.9 %collective-permute-start.14 = (bf16[96,384]{1,0:T(8,128)(2,1)S(1)}, bf16[96,384]{1,0:T(8,128)(2,1)S(1)}, u32[]{:S(2)}, u32[]{:S(2)}) collective-permute-start(bf16[96,384]{1,0:T(8,128)(2,1)S(1)} %get-tuple-element.67), channel_id=1, source_target_pairs={{0,16},{8,24},{16,0},{24,8},{1,17},{9,25},{17,1},{25,9},{2,18},{10... | collective-permute-start | bytes 221192 | tf_op jit(solution)/shard_map/ppermute | solution.py:356
  43.7 9.3 %collective-permute-start.15 = (bf16[96,384]{1,0:T(8,128)(2,1)S(1)}, bf16[96,384]{1,0:T(8,128)(2,1)S(1)}, u32[]{:S(2)}, u32[]{:S(2)}) collective-permute-start(bf16[96,384]{1,0:T(8,128)(2,1)S(1)} %get-tuple-element.68), channel_id=1, source_target_pairs={{0,24},{8,16},{16,8},{24,0},{1,25},{9,17},{17,9},{25,1},{2,26},{10... | collective-permute-start | bytes 221192 | tf_op jit(solution)/shard_map/ppermute | solution.py:356

commit v3 on v2

v3 whole, which is shorter than its diff:
```python
import functools

import jax
import jax.numpy as jnp
from jax import lax
from jax.experimental import pallas as pl
from jax.experimental.pallas import tpu as pltpu
from jax.sharding import PartitionSpec as P


LANES = 128
GRAIN = 8
STEP = 2
VMEM_BYTES = 67043328
SLACK = 12*2**20
SMALL = 4 * 2**20
PARTS = (1, 1)


def parts_of(p_own):
    if p_own % sum(PARTS):
        return (p_own,)
    return tuple(p_own // sum(PARTS) * part for part in PARTS)


STAGES = (("one", ((1, 0), (1, 1))), ("two", ((0, 1),)), ("own", ((0, 0),)))


def rows_of_stages(dims, chunk):
    general, active, gen_size, act_size = dims
    size = 2 * parts_of(general // gen_size)[chunk] * (active // act_size)
    found, row = {}, 0
    for name, members in STAGES:
        found[name] = (row, row + size * len(members))
        row += size * len(members)
    return found, row


def halves_of(ranges, half):
    first = ranges["one"][1]
    return (0, first), (first, half)


def make_weights(dims, chunk, t, column, bra_pack, ket_pack, weights):
    general, active, gen_size, act_size = dims
    p_own, u_own = general // gen_size, active // act_size
    parts = parts_of(p_own)
    p_from = sum(parts[:chunk])
    size = parts[chunk] * u_own
    order = [member for _, members in STAGES for member in members]
    me_gen, me_act = lax.axis_index("gen"), lax.axis_index("act")
    left, right = slice(column, column + LANES), slice(column + LANES, column + 2 * LANES)
    row = 0
    for core in (1, 0):
        odd = (me_gen & 1) ^ core
        for first, second in order:
            q = jnp.where(odd == 1, first, second)
            a = jnp.where(odd == 1, second, first)
            p_first = (me_gen ^ (2 * q + core)) * p_own + p_from
            u_first = pl.multiple_of((me_act ^ a) * u_own, 8)
            ket_re = ket_pack[t, pl.ds(u_first, u_own), :]
            ket_im = ket_pack[t, pl.ds(active + u_first, u_own), :]
            real, imag = [], []
            for p in range(parts[chunk]):
                bra_re = bra_pack[t, pl.ds(p_first + p, 1), :]
                bra_im = bra_pack[t, pl.ds(general + p_first + p, 1), :]
                real.append(bra_re * ket_re + bra_im * ket_im)
                imag.append(bra_re * ket_im - bra_im * ket_re)
            real = jnp.concatenate(real, axis=0)
            imag = jnp.concatenate(imag, axis=0)
            real_low = real.astype(jnp.bfloat16)
            weights[row : row + size, left] = real_low
            weights[row : row + size, right] = (-imag).astype(jnp.bfloat16)
            row += size
            weights[row : row + size, left] = imag.astype(jnp.bfloat16)
            weights[row : row + size, right] = real_low
            row += size


def accumulate(dims, chunk, tiles, packed, bra_pack, ket_pack, weights, acc, results, arrive):
    def product(first, count, state):
        for k in range(count):
            make_weights(dims, chunk, first + k, 2 * LANES * k, bra_pack, ket_pack, weights)
        state = arrive(first + count, state)
        values = []
        for k in range(count):
            row = pl.multiple_of((first + k) * LANES, LANES)
            values.append(packed[0, pl.ds(row, LANES), :])
            values.append(packed[1, pl.ds(row, LANES), :])
        values = jnp.concatenate(values, axis=0)
        left = weights[:, : 2 * LANES * count]
        return jnp.dot(left, values, preferred_element_type=jnp.float32), state

    def step(i, state):
        value, state = product(i * STEP, STEP, state)
        acc[...] += value
        return state

    steps = (tiles - 1) // STEP

    def opening(state):
        value, state = product(0, STEP, state)
        acc[...] = value
        return state

    def empty(state):
        acc[...] = jnp.zeros_like(acc)
        return state

    state = lax.cond(steps > 0, opening, empty, 0)
    state = lax.fori_loop(1, steps, step, state)
    for count in range(1, STEP + 1):
        @pl.when(tiles - steps * STEP == count)
        def _():
            value, _ = product(steps * STEP, count, state)
            value = acc[...] + value
            row = 0
            for result in results:
                result[...] = value[row : row + result.shape[0]].astype(result.dtype)
                row += result.shape[0]


def head_kernel(dims, blocks, width, counts, rows_ref, ints_ref, *refs):
    *results, packed, bra_pack, ket_pack = refs[:-4]
    weights, acc, offsets, sems = refs[-4:]
    general = dims[0]
    live = counts[blocks]

    def rows_of(b):
        return (counts[b] + GRAIN - 1) // GRAIN * GRAIN

    pieces = []
    size = width
    while size >= GRAIN:
        pieces.append(size)
        size //= 2

    def copies(b, act):
        rows = rows_of(b)
        start = pl.multiple_of(offsets[b], GRAIN)
        for piece in pieces:
            @pl.when((rows & piece) != 0)
            def _():
                first = pl.multiple_of(rows & ~(2 * piece - 1), GRAIN)
                copy = pltpu.make_async_copy(
                    ints_ref.at[b, :, pl.ds(first, piece), :],
                    packed.at[:, pl.ds(start + first, piece), :],
                    sems.at[b],
                )
                act(copy)

    def place(b, total):
        offsets[b] = total
        copies(b, lambda c: c.start())
        return total + rows_of(b)

    total = lax.fori_loop(0, live, place, 0)
    tiles = (total + LANES - 1) // LANES

    def clear(i, _):
        row = pl.multiple_of(total + i * GRAIN, GRAIN)
        packed[:, pl.ds(row, GRAIN), :] = jnp.zeros((2, GRAIN, packed.shape[2]), packed.dtype)
        return 0

    lax.fori_loop(0, (tiles * LANES - total) // GRAIN, clear, 0)

    @pl.loop(0, tiles + 1)
    def _(t):
        bra_pack[t] = jnp.zeros(bra_pack.shape[1:], jnp.float32)
        ket_pack[t] = jnp.zeros(ket_pack.shape[1:], jnp.float32)

    lane = lax.broadcasted_iota(jnp.int32, (1, LANES), 1)
    for b in range(blocks):
        start = jnp.where(b < live, offsets[b], 0)
        rows = jnp.where(b < live, counts[b], 0)
        tile = start // LANES
        turn = start % LANES
        both = rows_ref[b].astype(jnp.float32)
        for first, last, target in ((0, general, bra_pack), (general, both.shape[1], ket_pack)):
            value = both[:, first:last].reshape(target.shape[1:])
            value = pltpu.roll(jnp.where(lane < rows, value, 0.0), turn, 1)
            target[tile] += jnp.where(lane >= turn, value, 0.0)
            target[tile + 1] += jnp.where(lane < turn, value, 0.0)

    def arrive(until, ready):
        def pending(b):
            start = offsets[jnp.minimum(b, blocks - 1)]
            return jnp.logical_and(b < live, start < until * LANES)

        def wait(b):
            copies(b, lambda c: c.wait())
            return b + 1

        return lax.while_loop(pending, wait, ready)

    accumulate(dims, 0, tiles, packed, bra_pack, ket_pack, weights, acc, results, arrive)


def tail_kernel(dims, chunk, blocks, counts, packed, bra_pack, ket_pack, *refs):
    *results, weights, acc = refs

    def add(b, total):
        return total + (counts[b] + GRAIN - 1) // GRAIN * GRAIN

    total = lax.fori_loop(0, counts[blocks], add, 0)
    accumulate(
        dims, chunk, (total + LANES - 1) // LANES, packed, bra_pack, ket_pack, weights, acc, results,
        lambda until, state: state,
    )


SMEM = pl.BlockSpec(memory_space=pltpu.SMEM)
VMEM = pl.BlockSpec(memory_space=pltpu.VMEM)
HBM = pl.BlockSpec(memory_space=pltpu.HBM)


def products(dims, chunk, counts, operands):
    general, active, _, _ = dims
    columns = operands[-1].shape[3] if chunk == 0 else operands[0].shape[2]
    blocks = counts.shape[0] - 1
    ranges, half = rows_of_stages(dims, chunk)
    rows = 2 * half
    outs = [
        jax.ShapeDtypeStruct((last - first, columns), jnp.bfloat16)
        for first, last in halves_of(ranges, half)
    ]
    outs += [
        jax.ShapeDtypeStruct((last - first, columns), jnp.float32)
        for first, last in ranges.values()
    ]
    out_specs = [VMEM] * len(outs)
    work = [
        pltpu.VMEM((rows, 2 * STEP * LANES), jnp.bfloat16),
        pltpu.VMEM((rows, columns), jnp.float32),
    ]
    cost = pl.CostEstimate(
        flops=rows * columns * 2 * blocks * LANES, bytes_accessed=rows * columns * 3, transcendentals=0
    )
    if chunk:
        return pl.pallas_call(
            functools.partial(tail_kernel, dims, chunk, blocks),
            out_shape=outs,
            in_specs=[SMEM, VMEM, VMEM, VMEM],
            out_specs=out_specs,
            scratch_shapes=work,
            compiler_params=pltpu.CompilerParams(vmem_limit_bytes=16 * 2**20),
            cost_estimate=cost,
        )(counts, *operands)
    _, integrals = operands
    width = integrals.shape[2]
    tiles = -(-blocks * width // LANES)
    outs += [
        jax.ShapeDtypeStruct((2, tiles * LANES, columns), jnp.bfloat16),
        jax.ShapeDtypeStruct((tiles + 1, 2 * general, LANES), jnp.float32),
        jax.ShapeDtypeStruct((tiles + 1, 2 * active, LANES), jnp.float32),
    ]
    grant = VMEM_BYTES - sum(x.size * x.dtype.itemsize for x in outs) - SLACK
    return pl.pallas_call(
        functools.partial(head_kernel, dims, blocks, width),
        out_shape=outs,
        in_specs=[SMEM, VMEM, HBM],
        out_specs=[VMEM] * len(outs),
        scratch_shapes=[
            *work,
            pltpu.SMEM((blocks,), jnp.int32),
            pltpu.SemaphoreType.DMA((blocks,)),
        ],
        compiler_params=pltpu.CompilerParams(vmem_limit_bytes=grant),
        cost_estimate=cost,
        name="products_0",
    )(counts, *operands)


def window_of(columns, parts):
    own = columns // parts
    starts = [own * a // LANES * LANES for a in range(parts)]
    ends = [-(-own * (a + 1) // LANES) * LANES for a in range(parts)]
    return own, max(e - s for s, e in zip(starts, ends))


def dense_rows(own, rows):
    full, rest = divmod(own, LANES)
    return full * rows + rows * rest // LANES


def small(kernel, outs, *operands):
    return pl.pallas_call(
        kernel,
        out_shape=outs,
        in_specs=[VMEM] * len(operands),
        out_specs=jax.tree.map(lambda _: VMEM, outs),
        compiler_params=pltpu.CompilerParams(vmem_limit_bytes=SMALL),
        cost_estimate=pl.CostEstimate(
            flops=sum(x.size for x in operands),
            bytes_accessed=4 * sum(x.size for x in operands),
            transcendentals=0,
        ),
    )(*operands)


def total_call(kernel, outs, shape, *operands):
    scratch = [pltpu.VMEM(shape, jnp.float32)] if outs else []
    outs = outs or [jax.ShapeDtypeStruct(shape, jnp.float32)]
    return pl.pallas_call(
        kernel,
        out_shape=outs,
        in_specs=[VMEM] * len(operands),
        out_specs=[VMEM] * len(outs),
        scratch_shapes=scratch,
        compiler_params=pltpu.CompilerParams(vmem_limit_bytes=SMALL),
        cost_estimate=pl.CostEstimate(
            flops=sum(x.size for x in operands),
            bytes_accessed=4 * sum(x.size for x in operands),
            transcendentals=0,
        ),
    )(*operands)


def wide(ref, ranges, name):
    first, last = ranges[name]
    base = ranges["one"][1] if name != "one" else 0
    first, last = first - base, last - base
    return ref[first:last].astype(jnp.float32)


def first_kernel(ranges, one_ref, got_ref, one_out):
    one_out[...] = (one_ref[...] + wide(got_ref, ranges, "one")).astype(one_out.dtype)


def second_kernel(ranges, two_ref, got_ref, from_one, two_out):
    size = two_ref.shape[0]
    value = two_ref[...] + wide(got_ref, ranges, "two") + from_one[size:].astype(jnp.float32)
    two_out[...] = value.astype(two_out.dtype)


def total_kernel(ranges, parts, own_ref, got_ref, from_one, from_two, *outs):
    total = outs[-1]
    value = own_ref[...] + wide(got_ref, ranges, "own")
    value = value + from_one[: own_ref.shape[0]].astype(jnp.float32)
    total[...] = value + from_two[...].astype(jnp.float32)
    if parts:
        rows, columns = total.shape
        own, width = window_of(columns, parts)
        full, rest = divmod(own, LANES)
        lane = lax.broadcasted_iota(jnp.int32, (1, LANES), 1)
        me = lax.axis_index("ao")
        for k, out in enumerate(outs[:-1]):
            first = jnp.minimum((me ^ k) * own // LANES * LANES, columns - width)
            shift = (me ^ k) * own - first
            cut = total[:, pl.ds(pl.multiple_of(first, LANES), width)]
            cut = pltpu.roll(cut, jnp.where(shift == 0, 0, width - shift), 1)
            parcels = [cut[:, j * LANES : (j + 1) * LANES] for j in range(full)]
            if rest:
                groups = LANES // rest
                size = rows // groups
                left = cut[:, full * LANES : (full + 1) * LANES]
                parcel = left[:size]
                for g in range(1, groups):
                    moved = pltpu.roll(left[g * size : (g + 1) * size], g * rest, 1)
                    parcel = jnp.where(lane >= g * rest, moved, parcel)
                parcels.append(parcel)
            out[...] = jnp.concatenate(parcels, axis=0).astype(out.dtype)


def final_kernel(parts, own, *refs):
    out_ref = refs[-1]
    u_own = out_ref.shape[2]
    full, rest = divmod(own, LANES)
    p_from = 0
    for j in range(len(refs) // parts):
        group = refs[j * parts : (j + 1) * parts]
        value = group[0][...]
        for ref in group[1:]:
            value = value + ref[...].astype(jnp.float32)
        rows = value.shape[0] * LANES // own
        pieces = [value[i * rows : (i + 1) * rows] for i in range(full)]
        if rest:
            left = value[full * rows :]
            turns = [left] + [
                pltpu.roll(left, LANES - g * rest, 1) for g in range(1, LANES // rest)
            ]
            pieces.append(jnp.concatenate(turns, axis=0))
        value = jnp.concatenate(pieces, axis=1)[:, :own]
        part = rows // (2 * u_own)
        out_ref[:, p_from : p_from + part] = value.reshape(2, part, u_own, own)
        p_from += part


def swap(size, bit):
    return [(i, i ^ bit) for i in range(size)]


def local(integrals, bra_rows, ket_rows, block_count, pair_count):
    columns = integrals.shape[3]
    general, active = bra_rows.shape[3], ket_rows.shape[3]
    ao_size = lax.axis_size("ao")
    gen_size = lax.axis_size("gen")
    act_size = lax.axis_size("act")
    bra = jnp.swapaxes(bra_rows, 2, 3)
    ket = jnp.swapaxes(ket_rows, 2, 3)
    p_own, u_own = general // gen_size, active // act_size
    dims = (general, active, gen_size, act_size)
    counts = jnp.concatenate([pair_count, block_count])
    operands = (jnp.concatenate([bra, ket], axis=2), integrals)
    own, _ = window_of(columns, ao_size)
    outs = []
    assert (gen_size, act_size) == (4, 2)
    for chunk, part in enumerate(parts_of(p_own)):
        block = 2 * part * u_own
        ranges, _ = rows_of_stages(dims, chunk)
        to_core, to_core_rest, *keep = products(dims, chunk, counts, operands)
        if chunk == 0:
            operands = tuple(keep[len(ranges) :])
        got = lax.ppermute(to_core, "gen", swap(gen_size, 1))
        rest = lax.ppermute(to_core_rest, "gen", swap(gen_size, 1))
        keep = dict(zip(ranges, keep))

        def move(value, axis, bit):
            return lax.ppermute(value, axis, swap(lax.axis_size(axis), bit))

        def cross(value, odd_first):
            def partner(g, k):
                return (g ^ 2, k) if g % 2 == odd_first else (g, k ^ 1)

            pairs = []
            for g in range(gen_size):
                for k in range(act_size):
                    to_g, to_k = partner(g, k)
                    pairs.append((g * act_size + k, to_g * act_size + to_k))
            return lax.ppermute(value, ("gen", "act"), pairs)

        to_one = small(
            functools.partial(first_kernel, ranges),
            jax.ShapeDtypeStruct(keep["one"].shape, jnp.bfloat16), keep["one"], got,
        )
        from_one = cross(to_one, 1)
        to_two = small(
            functools.partial(second_kernel, ranges),
            jax.ShapeDtypeStruct(keep["two"].shape, jnp.bfloat16), keep["two"], rest, from_one,
        )
        from_two = cross(to_two, 0)
        parts = ao_size if ao_size <= 4 else 0
        if parts:
            totals = [
                jax.ShapeDtypeStruct(
                    (dense_rows(own, block), LANES), jnp.bfloat16 if k else jnp.float32
                )
                for k in range(parts)
            ]
        else:
            totals = []
        windows = total_call(
            functools.partial(total_kernel, ranges, parts), totals,
            (block, columns), keep["own"], rest, from_one, from_two,
        )
        if parts:
            outs.append(windows[0])
            outs += [move(windows[k], "ao", k) for k in range(1, parts)]
        else:
            total = windows[0].reshape(block, ao_size, own)
            total = jnp.swapaxes(total, 0, 1).reshape(ao_size * block, own)
            value = lax.psum_scatter(total, "ao", scatter_dimension=0, tiled=True)
            outs.append(value.reshape(2, part, u_own, own))
    if parts:
        result = jax.ShapeDtypeStruct((2, p_own, u_own, own), jnp.float32)
        return small(functools.partial(final_kernel, parts, own), result, *outs)
    return jnp.concatenate(outs, axis=1)


def solution(mesh):
    spec = P(("ao", "gen", "act"), None, None, None)
    count = P(("ao", "gen", "act"))

    def program(integrals, bra_rows, ket_rows, block_count, pair_count):
        mapped = jax.shard_map(
            local,
            mesh=mesh,
            in_specs=(spec, spec, spec, count, count),
            out_specs=P(None, "gen", "act", "ao"),
            check_vma=False,
        )
        return mapped(integrals, bra_rows, ket_rows, block_count, pair_count)

    return program
```

time: 54.1 us -> 48.9 us (0.904)
  starting transfers between devices: 23.5 us -> 20.7 us
  waiting for transfers between devices: 17.4 us -> 15.7 us
  Pallas kernels: 10.5 us -> 9.77 us
    ppermute x14 -> x6, waiting for transfers between devices: 17.4 us -> 2.72 us  [move(): return lax.ppermute(value, axis, swap(lax.axis_size(axis), bit))]
    ppermute x2 -> x8, waiting for transfers between devices: 0.01 us -> 13 us  [the longest x4 13 us: cross(): return lax.ppermute(value, ('gen', 'act'), pairs)]
    ppermute x14 -> x6, starting transfers between devices: 19.8 us -> 8.78 us  [move(): return lax.ppermute(value, axis, swap(lax.axis_size(axis), bit))]
    ppermute x2 -> x8, starting transfers between devices: 3.71 us -> 11.9 us  [the longest x4 8.56 us: cross(): return lax.ppermute(value, ('gen', 'act'), pairs)]
    pallas_call x2, Pallas kernels: 8.99 us -> 7.8 us  [the longest x1 4.72 us: products(): pl.pallas_call(functools.partial(head_kernel, dims, blocks, width), out_s...]
  transfers between devices with their start and end apart: 16 -> 14, of which waited for: 8 -> 6; matrix products, arithmetic and copies ran while one was open for 0% -> 0% of each run, Pallas kernels for 10% -> 9%
where the time goes in v3:
time: 48.9 us; the launch traced here: 48.7 us
  starting transfers between devices  20.7 us (42%)
  waiting for transfers between devices  15.7 us (32%)
  Pallas kernels  9.77 us (20%)
  other arithmetic  1.75 us (4%)
  between operations  0.77 us (2%)
    ppermute x4, waiting for transfers between devices, cross(): return lax.ppermute(value, ('gen', 'act'), pairs)  13 us
    ppermute x6, starting transfers between devices, move(): return lax.ppermute(value, axis, swap(lax.axis_size(axis), bit))  8.78 us
    ppermute x4, starting transfers between devices, cross(): return lax.ppermute(value, ('gen', 'act'), pairs)  8.56 us
    pallas_call x1, Pallas kernels, products(): pl.pallas_call(functools.partial(head_kernel, dims, blocks, width), out_s...  4.72 us
    ppermute x2, starting transfers between devices, local(): got = lax.ppermute(to_core, 'gen', swap(gen_size, 1))  3.26 us
    pallas_call x1, Pallas kernels, products(): pl.pallas_call(functools.partial(tail_kernel, dims, chunk, blocks), out_s...  3.09 us
    ppermute x6, waiting for transfers between devices, move(): return lax.ppermute(value, axis, swap(lax.axis_size(axis), bit))  2.72 us
    pallas_call x5, Pallas kernels, small(): pl.pallas_call(kernel, out_shape=outs, in_specs=[VMEM] * len(operands), o...  1.15 us
  transfers between devices with their start and end apart: 14, of which 6 were waited for; matrix products, arithmetic and copies ran while one was open for 0% of the time, Pallas kernels for 9%

profile of v3, /device:TPU:0, one launch (start us, length us, event | category | flops | bytes accessed | tf_op | source)
XLA Modules:
  0.0 48.7 jit_solution(8867204096751502515)
XLA Ops:
  0.7 0.7 %pad_add_fusion.counts = s32[13]{0:T(128)S(1)} fusion(s32[1]{0:T(128)S(6)} %copy.6, s32[12]{0:T(128)} %param.9), kind=kLoop, calls=%fused_computation.1 | loop fusion | flops 13 | bytes 104 | tf_op jit(solution)/shard_map/concatenate | solution.py:403
  1.4 1.0 %pad_maximum_fusion.rows_ref = bf16[12,2,64,128]{3,2,1,0:T(8,128)(2,1)S(1)} fusion(bf16[12,2,48,128]{3,2,1,0:T(8,128)(2,1)} %bitcast.2, bf16[12,2,16,128]{3,2,1,0:T(8,128)(2,1)} %bitcast.3), kind=kLoop, calls=%fused_computation | loop fusion | flops 786432 | bytes 786432 | tf_op jit(solution)/shard_map/concatenate | solution.py:404
  2.4 4.7 %products_0.1 = (bf16[192,1152]{1,0:T(8,128)(2,1)S(1)}, bf16[192,1152]{1,0:T(8,128)(2,1)S(1)}, f32[192,1152]{1,0:T(8,128)S(1)}, f32[96,1152]{1,0:T(8,128)S(1)}, ...) custom-call(s32[13]{0:T(128)S(1)} %pad_add_fusion.counts, ...), custom_call_target="tpu_custom_call" | custom-call | flops 2717908992 | bytes 2654208 | tf_op jit(solution)/shard_map/products_0/pallas_call | solution.py:258
  7.1 1.9 %collective-permute-start.1 = (bf16[192,1152]{1,0:T(8,128)(2,1)S(1)}, bf16[192,1152]{1,0:T(8,128)(2,1)S(1)}, u32[]{:S(2)}, u32[]{:S(2)}) collective-permute-start(bf16[192,1152]{1,0:T(8,128)(2,1)S(1)} %get-tuple-element.29), channel_id=1, source_target_pairs={{0,2},{2,0},{4,6},{6,4},{1,3},{3,1},{5,7},{7,5},{8,10},{10,8},{12,... | collective-permute-start | bytes 1327112 | tf_op jit(solution)/shard_map/ppermute | solution.py:414
  9.1 3.1 %shard_map.58 = (bf16[192,1152]{1,0:T(8,128)(2,1)S(1)}, bf16[192,1152]{1,0:T(8,128)(2,1)S(1)}, f32[192,1152]{1,0:T(8,128)S(1)}, f32[96,1152]{1,0:T(8,128)S(1)}, f32[96,1152]{1,0:T(8,128)S(1)}) custom-call(s32[13]{0:T(128)S(1)} %pad_add_fusion.counts, bf16[2,1536,1152]{2,1,0:T(8,128)(2,1)S(1)} %get-tuple-element.35.packed, ...), custom_call_target="tpu_custom_call" | custom-call | flops 2717908992 | bytes 2654208 | tf_op jit(solution)/shard_map/pallas_call | solution.py:240
  12.2 1.3 %collective-permute-start.8 = (bf16[192,1152]{1,0:T(8,128)(2,1)S(1)}, bf16[192,1152]{1,0:T(8,128)(2,1)S(1)}, u32[]{:S(2)}, u32[]{:S(2)}) collective-permute-start(bf16[192,1152]{1,0:T(8,128)(2,1)S(1)} %get-tuple-element.41), channel_id=1, source_target_pairs={{0,2},{2,0},{4,6},{6,4},{1,3},{3,1},{5,7},{7,5},{8,10},{10,8},{12,... | collective-permute-start | bytes 1327112 | tf_op jit(solution)/shard_map/ppermute | solution.py:414
  13.5 0.1 collective-permute-start
  13.6 0.1 shard_map.55
  13.6 7.2 %collective-permute-start.2 = (bf16[192,1152]{1,0:T(8,128)(2,1)S(1)}, bf16[192,1152]{1,0:T(8,128)(2,1)S(1)}, u32[]{:S(2)}, u32[]{:S(2)}) collective-permute-start(bf16[192,1152]{1,0:T(8,128)(2,1)S(1)} %shard_map.55), channel_id=1, source_target_pairs={{0,1},{1,0},{2,6},{3,7},{4,5},{5,4},{6,2},{7,3},{8,9},{9,8},{10,14... | collective-permute-start | bytes 1327112 | tf_op jit(solution)/shard_map/ppermute | solution.py:430
  20.9 0.1 shard_map.59
  21.0 1.2 %collective-permute-start.9 = (bf16[192,1152]{1,0:T(8,128)(2,1)S(1)}, bf16[192,1152]{1,0:T(8,128)(2,1)S(1)}, u32[]{:S(2)}, u32[]{:S(2)}) collective-permute-start(bf16[192,1152]{1,0:T(8,128)(2,1)S(1)} %shard_map.59), channel_id=1, source_target_pairs={{0,1},{1,0},{2,6},{3,7},{4,5},{5,4},{6,2},{7,3},{8,9},{9,8},{10,14... | collective-permute-start | bytes 1327112 | tf_op jit(solution)/shard_map/ppermute | solution.py:430
  22.2 0.0 collective-permute-done.got_ref
  22.2 5.0 %collective-permute-done.2.from_one = bf16[192,1152]{1,0:T(8,128)(2,1)S(1)} collective-permute-done((bf16[192,1152]{1,0:T(8,128)(2,1)S(1)}, bf16[192,1152]{1,0:T(8,128)(2,1)S(1)}, u32[]{:S(2)}, u32[]{:S(2)}) %collective-permute-start.2) | collective-permute-done | bytes 442400 | tf_op jit(solution)/shard_map/ppermute | solution.py:430
  27.2 0.1 shard_map.56
  27.2 0.1 collective-permute-start.3
  27.3 0.0 collective-permute-done.7.got_ref
  27.3 6.9 %collective-permute-done.9.from_one = bf16[192,1152]{1,0:T(8,128)(2,1)S(1)} collective-permute-done((bf16[192,1152]{1,0:T(8,128)(2,1)S(1)}, bf16[192,1152]{1,0:T(8,128)(2,1)S(1)}, u32[]{:S(2)}, u32[]{:S(2)}) %collective-permute-start.9) | collective-permute-done | bytes 442400 | tf_op jit(solution)/shard_map/ppermute | solution.py:430
  34.3 0.1 shard_map.60
  34.4 0.1 collective-permute-start.10
  34.4 0.4 shard_map.57
  34.9 0.0 collective-permute-start.4
  34.9 0.1 collective-permute-start.5
  35.0 4.3 %collective-permute-start.6 = (bf16[216,128]{1,0:T(8,128)(2,1)S(1)}, bf16[216,128]{1,0:T(8,128)(2,1)S(1)}, u32[]{:S(2)}, u32[]{:S(2)}) collective-permute-start(bf16[216,128]{1,0:T(8,128)(2,1)S(1)} %get-tuple-element.34), channel_id=1, source_target_pairs={{0,24},{8,16},{16,8},{24,0},{1,25},{9,17},{17,9},{25,1},{2,26},{10... | collective-permute-start | bytes 165896 | tf_op jit(solution)/shard_map/ppermute | solution.py:419
  39.3 1.1 %collective-permute-done.10.from_two = bf16[96,1152]{1,0:T(8,128)(2,1)S(1)} collective-permute-done((bf16[96,1152]{1,0:T(8,128)(2,1)S(1)}, bf16[96,1152]{1,0:T(8,128)(2,1)S(1)}, u32[]{:S(2)}, u32[]{:S(2)}) %collective-permute-start.10) | collective-permute-done | bytes 221216 | tf_op jit(solution)/shard_map/ppermute | solution.py:430
  40.4 0.4 shard_map.61
  40.8 0.0 collective-permute-start.11
  40.8 0.1 collective-permute-start.12
  40.9 4.3 %collective-permute-start.13 = (bf16[216,128]{1,0:T(8,128)(2,1)S(1)}, bf16[216,128]{1,0:T(8,128)(2,1)S(1)}, u32[]{:S(2)}, u32[]{:S(2)}) collective-permute-start(bf16[216,128]{1,0:T(8,128)(2,1)S(1)} %get-tuple-element.46), channel_id=1, source_target_pairs={{0,24},{8,16},{16,8},{24,0},{1,25},{9,17},{17,9},{25,1},{2,26},{10... | collective-permute-start | bytes 165896 | tf_op jit(solution)/shard_map/ppermute | solution.py:419
  45.2 0.1 collective-permute-done.11.refs_5_
  45.3 0.7 %collective-permute-done.12.refs_6_ = bf16[216,128]{1,0:T(8,128)(2,1)S(1)} collective-permute-done((bf16[216,128]{1,0:T(8,128)(2,1)S(1)}, bf16[216,128]{1,0:T(8,128)(2,1)S(1)}, u32[]{:S(2)}, u32[]{:S(2)}) %collective-permute-start.12) | collective-permute-done | bytes 55328 | tf_op jit(solution)/shard_map/ppermute | solution.py:419
  46.0 1.9 %collective-permute-done.13.refs_7_ = bf16[216,128]{1,0:T(8,128)(2,1)S(1)} collective-permute-done((bf16[216,128]{1,0:T(8,128)(2,1)S(1)}, bf16[216,128]{1,0:T(8,128)(2,1)S(1)}, u32[]{:S(2)}, u32[]{:S(2)}) %collective-permute-start.13) | collective-permute-done | bytes 55328 | tf_op jit(solution)/shard_map/ppermute | solution.py:419
  47.9 0.8 %shard_map.62 = f32[2,4,24,288]{3,2,1,0:T(8,128)} custom-call(f32[216,128]{1,0:T(8,128)S(1)} %get-tuple-element.31.refs_0_, bf16[216,128]{1,0:T(8,128)(2,1)S(1)} %collective-permute-done.4.refs_1_, bf16[216,128]{1,0:T(8,128)(2,1)S(1)} %collective-permute-done.5.refs_2_, bf16[216,128]{1,0:T(8,128)(2,1)S(1)} %collective-permute-done.6.refs_3_, ...), custom_call_target="tpu_custom_call" | custom-call | flops 221184 | bytes 884736 | tf_op jit(solution)/shard_map/pallas_call | solution.py:287
  (7 shorter events, 0.0 us)
Async XLA Ops:
  7.1 6.4 %collective-permute-start.1 = (bf16[192,1152]{1,0:T(8,128)(2,1)S(1)}, bf16[192,1152]{1,0:T(8,128)(2,1)S(1)}, u32[]{:S(2)}, u32[]{:S(2)}) collective-permute-start(bf16[192,1152]{1,0:T(8,128)(2,1)S(1)} %get-tuple-element.29), channel_id=1, source_target_pairs={{0,2},{2,0},{4,6},{6,4},{1,3},{3,1},{5,7},{7,5},{8,10},{10,8},{12,... | collective-permute-start | bytes 1327112 | tf_op jit(solution)/shard_map/ppermute | solution.py:414
  12.2 8.7 %collective-permute-start.8 = (bf16[192,1152]{1,0:T(8,128)(2,1)S(1)}, bf16[192,1152]{1,0:T(8,128)(2,1)S(1)}, u32[]{:S(2)}, u32[]{:S(2)}) collective-permute-start(bf16[192,1152]{1,0:T(8,128)(2,1)S(1)} %get-tuple-element.41), channel_id=1, source_target_pairs={{0,2},{2,0},{4,6},{6,4},{1,3},{3,1},{5,7},{7,5},{8,10},{10,8},{12,... | collective-permute-start | bytes 1327112 | tf_op jit(solution)/shard_map/ppermute | solution.py:414
  13.5 8.7 %collective-permute-start = (bf16[192,1152]{1,0:T(8,128)(2,1)S(1)}, bf16[192,1152]{1,0:T(8,128)(2,1)S(1)}, u32[]{:S(2)}, u32[]{:S(2)}) collective-permute-start(bf16[192,1152]{1,0:T(8,128)(2,1)S(1)} %get-tuple-element.27), channel_id=1, source_target_pairs={{0,2},{2,0},{4,6},{6,4},{1,3},{3,1},{5,7},{7,5},{8,10},{10,8},{12,... | collective-permute-start | bytes 1327112 | tf_op jit(solution)/shard_map/ppermute | solution.py:415
  13.6 13.5 %collective-permute-start.2 = (bf16[192,1152]{1,0:T(8,128)(2,1)S(1)}, bf16[192,1152]{1,0:T(8,128)(2,1)S(1)}, u32[]{:S(2)}, u32[]{:S(2)}) collective-permute-start(bf16[192,1152]{1,0:T(8,128)(2,1)S(1)} %shard_map.55), channel_id=1, source_target_pairs={{0,1},{1,0},{2,6},{3,7},{4,5},{5,4},{6,2},{7,3},{8,9},{9,8},{10,14... | collective-permute-start | bytes 1327112 | tf_op jit(solution)/shard_map/ppermute | solution.py:430
  20.9 6.5 %collective-permute-start.7 = (bf16[192,1152]{1,0:T(8,128)(2,1)S(1)}, bf16[192,1152]{1,0:T(8,128)(2,1)S(1)}, u32[]{:S(2)}, u32[]{:S(2)}) collective-permute-start(bf16[192,1152]{1,0:T(8,128)(2,1)S(1)} %get-tuple-element.39), channel_id=1, source_target_pairs={{0,2},{2,0},{4,6},{6,4},{1,3},{3,1},{5,7},{7,5},{8,10},{10,8},{12,... | collective-permute-start | bytes 1327112 | tf_op jit(solution)/shard_map/ppermute | solution.py:415
  21.0 13.3 %collective-permute-start.9 = (bf16[192,1152]{1,0:T(8,128)(2,1)S(1)}, bf16[192,1152]{1,0:T(8,128)(2,1)S(1)}, u32[]{:S(2)}, u32[]{:S(2)}) collective-permute-start(bf16[192,1152]{1,0:T(8,128)(2,1)S(1)} %shard_map.59), channel_id=1, source_target_pairs={{0,1},{1,0},{2,6},{3,7},{4,5},{5,4},{6,2},{7,3},{8,9},{9,8},{10,14... | collective-permute-start | bytes 1327112 | tf_op jit(solution)/shard_map/ppermute | solution.py:430
  27.2 7.2 %collective-permute-start.3 = (bf16[96,1152]{1,0:T(8,128)(2,1)S(1)}, bf16[96,1152]{1,0:T(8,128)(2,1)S(1)}, u32[]{:S(2)}, u32[]{:S(2)}) collective-permute-start(bf16[96,1152]{1,0:T(8,128)(2,1)S(1)} %shard_map.56), channel_id=1, source_target_pairs={{0,4},{1,5},{2,3},{3,2},{4,0},{5,1},{6,7},{7,6},{8,12},{9,13},{10,... | collective-permute-start | bytes 663560 | tf_op jit(solution)/shard_map/ppermute | solution.py:430
  34.4 6.0 %collective-permute-start.10 = (bf16[96,1152]{1,0:T(8,128)(2,1)S(1)}, bf16[96,1152]{1,0:T(8,128)(2,1)S(1)}, u32[]{:S(2)}, u32[]{:S(2)}) collective-permute-start(bf16[96,1152]{1,0:T(8,128)(2,1)S(1)} %shard_map.60), channel_id=1, source_target_pairs={{0,4},{1,5},{2,3},{3,2},{4,0},{5,1},{6,7},{7,6},{8,12},{9,13},{10,... | collective-permute-start | bytes 663560 | tf_op jit(solution)/shard_map/ppermute | solution.py:430
  34.9 6.0 %collective-permute-start.4 = (bf16[216,128]{1,0:T(8,128)(2,1)S(1)}, bf16[216,128]{1,0:T(8,128)(2,1)S(1)}, u32[]{:S(2)}, u32[]{:S(2)}) collective-permute-start(bf16[216,128]{1,0:T(8,128)(2,1)S(1)} %get-tuple-element.32), channel_id=1, source_target_pairs={{0,8},{8,0},{16,24},{24,16},{1,9},{9,1},{17,25},{25,17},{2,10},{10... | collective-permute-start | bytes 165896 | tf_op jit(solution)/shard_map/ppermute | solution.py:419
  34.9 10.3 %collective-permute-start.5 = (bf16[216,128]{1,0:T(8,128)(2,1)S(1)}, bf16[216,128]{1,0:T(8,128)(2,1)S(1)}, u32[]{:S(2)}, u32[]{:S(2)}) collective-permute-start(bf16[216,128]{1,0:T(8,128)(2,1)S(1)} %get-tuple-element.33), channel_id=1, source_target_pairs={{0,16},{8,24},{16,0},{24,8},{1,17},{9,25},{17,1},{25,9},{2,18},{10... | collective-permute-start | bytes 165896 | tf_op jit(solution)/shard_map/ppermute | solution.py:419
  35.0 10.2 %collective-permute-start.6 = (bf16[216,128]{1,0:T(8,128)(2,1)S(1)}, bf16[216,128]{1,0:T(8,128)(2,1)S(1)}, u32[]{:S(2)}, u32[]{:S(2)}) collective-permute-start(bf16[216,128]{1,0:T(8,128)(2,1)S(1)} %get-tuple-element.34), channel_id=1, source_target_pairs={{0,24},{8,16},{16,8},{24,0},{1,25},{9,17},{17,9},{25,1},{2,26},{10... | collective-permute-start | bytes 165896 | tf_op jit(solution)/shard_map/ppermute | solution.py:419
  40.8 4.5 %collective-permute-start.11 = (bf16[216,128]{1,0:T(8,128)(2,1)S(1)}, bf16[216,128]{1,0:T(8,128)(2,1)S(1)}, u32[]{:S(2)}, u32[]{:S(2)}) collective-permute-start(bf16[216,128]{1,0:T(8,128)(2,1)S(1)} %get-tuple-element.44), channel_id=1, source_target_pairs={{0,8},{8,0},{16,24},{24,16},{1,9},{9,1},{17,25},{25,17},{2,10},{10... | collective-permute-start | bytes 165896 | tf_op jit(solution)/shard_map/ppermute | solution.py:419
  40.8 5.2 %collective-permute-start.12 = (bf16[216,128]{1,0:T(8,128)(2,1)S(1)}, bf16[216,128]{1,0:T(8,128)(2,1)S(1)}, u32[]{:S(2)}, u32[]{:S(2)}) collective-permute-start(bf16[216,128]{1,0:T(8,128)(2,1)S(1)} %get-tuple-element.45), channel_id=1, source_target_pairs={{0,16},{8,24},{16,0},{24,8},{1,17},{9,25},{17,1},{25,9},{2,18},{10... | collective-permute-start | bytes 165896 | tf_op jit(solution)/shard_map/ppermute | solution.py:419
  40.9 7.0 %collective-permute-start.13 = (bf16[216,128]{1,0:T(8,128)(2,1)S(1)}, bf16[216,128]{1,0:T(8,128)(2,1)S(1)}, u32[]{:S(2)}, u32[]{:S(2)}) collective-permute-start(bf16[216,128]{1,0:T(8,128)(2,1)S(1)} %get-tuple-element.46), channel_id=1, source_target_pairs={{0,24},{8,16},{16,8},{24,0},{1,25},{9,17},{17,9},{25,1},{2,26},{10... | collective-permute-start | bytes 165896 | tf_op jit(solution)/shard_map/ppermute | solution.py:419
